TPU v7x, 32 devices: a whole 2x2x4 slice. The times are simulated.
32 devices in a mesh: group: 2 (over y), visit: 16 (over z, x, core), sky: 1.
Axes of the slice: x: 2, y: 2, z: 4, core: 2. Of those that a mesh axis runs over, the one named last changes fastest.
Arguments:
- template: bfloat16 [64, 128], P(('group', 'visit'), 'sky'), parts along dimension 0, may hold values from -6 to 6
- science: float32 [32, 32, 128], P(('group', 'visit'), None, 'sky'), parts along dimension 0, may hold values from -15 to 15
- variance: float32 [32, 32, 128], P(('group', 'visit'), None, 'sky'), parts along dimension 0, may hold values from 0.5 to 4
- col_taps: bfloat16 [49, 31], replicated, may hold values from -1 to 1
- row_taps: bfloat16 [49, 31], replicated, may hold values from -1 to 1
- stamp_rows: int32 [32, 1, 16], P(('group', 'visit'), 'sky'), parts along dimension 0, may hold values from 0 to 16
- stamp_cols: int32 [32, 1, 16], P(('group', 'visit'), 'sky'), parts along dimension 0, may hold values from 0 to 112
Outputs:
- difference: float32 [32, 32, 128], P(('group', 'visit'), None, 'sky'), parts along dimension 0
- coefficients: float32 [32, 50], P(('group', 'visit')), parts along dimension 0
- detection: float32 [64, 128], P(('group', 'visit'), 'sky'), parts along dimension 0
There are 2 independent parts, one for each index of `group`. A program takes and returns all parts, laid end to end along the dimension named above; an argument that names none is the same for every part. Nothing has to cross between parts.
All inputs are finite; a program needn't handle non-finite values.
Results may differ from a plain program's by a relative error of at most 0.0018.
Values may be sent and summed in bfloat16 or wider, within the bound.
No kernel may reach another device: no remote copies, remote signals or barrier semaphores. Data moves between devices by JAX's collectives and lax.ppermute only.
A program may use at most 128 MiB of HBM per device.

v0:
```python
import jax
import jax.numpy as jnp
from jax import lax
from jax.sharding import PartitionSpec as P

KBLK = 7
STAMP = 16


def with_halo(cells, sides, width):
    for axis, dim in sides:
        count = lax.axis_size(axis)
        ends = count - 1
        head = lax.slice_in_dim(cells, 0, width, axis=dim)
        tail = lax.slice_in_dim(cells, cells.shape[dim] - width, cells.shape[dim], axis=dim)
        cells = jnp.concatenate(
            [
                lax.ppermute(tail, axis, [(i, (i + 1) % count) for i in range(ends)]),
                cells,
                lax.ppermute(head, axis, [((i + 1) % count, i) for i in range(ends)]),
            ],
            axis=dim,
        )
    return cells


def tap_selectors(out_len, in_len, tap_count):
    offsets = (
        jnp.arange(in_len, dtype=jnp.int32)[None, :] - jnp.arange(out_len, dtype=jnp.int32)[:, None]
    )
    return (offsets[None, :, :] == jnp.arange(tap_count, dtype=jnp.int32)[:, None, None]).astype(
        jnp.float32
    )


def column_pass(padded, taps_block):
    tap_count = taps_block.shape[1]
    out_width = padded.shape[1] - tap_count + 1
    selectors = tap_selectors(out_width, padded.shape[1], tap_count)
    band_mats = jnp.einsum("kj,jci->kic", taps_block.astype(jnp.float32), selectors).astype(
        jnp.bfloat16
    )
    result = jnp.einsum("ri,kic->krc", padded, band_mats, preferred_element_type=jnp.float32)
    return result.astype(jnp.bfloat16)


def band_matrix(taps_block, out_len, in_len):
    tap_count = taps_block.shape[1]
    offsets = (
        jnp.arange(in_len, dtype=jnp.int32)[None, :] - jnp.arange(out_len, dtype=jnp.int32)[:, None]
    )
    taps_wide = taps_block.astype(jnp.float32)
    band = jnp.zeros((taps_block.shape[0], out_len, in_len), jnp.float32)
    for offset in range(tap_count):
        band = band + jnp.where(
            offsets[None, :, :] == offset, taps_wide[:, offset][:, None, None], 0.0
        )
    return band.astype(jnp.bfloat16)


def row_pass(columns, taps_block):
    tap_count = taps_block.shape[1]
    margin = (tap_count - 1) // 2
    height = columns.shape[1]
    stride = min(512, height)
    padded = jnp.pad(columns, ((0, 0), (margin, margin), (0, 0)))
    band = band_matrix(taps_block, stride, stride + 2 * margin)
    pieces = jnp.einsum("kti,kiw->ktw", band, padded, preferred_element_type=jnp.float32).astype(
        jnp.bfloat16
    )
    return pieces


def extract_stamps(block, row_starts, col_starts):

    def extract(row_start, col_start):
        return lax.dynamic_slice(
            block, (jnp.int32(0), row_start, col_start), (block.shape[0], STAMP, STAMP)
        )

    stamps = jax.vmap(extract)(row_starts, col_starts)
    return jnp.transpose(stamps, (1, 0, 2, 3)).reshape(block.shape[0], -1)


def extract_plane(plane, row_starts, col_starts):

    def extract(row_start, col_start):
        return lax.dynamic_slice(plane, (row_start, col_start), (STAMP, STAMP))

    return jax.vmap(extract)(row_starts, col_starts).reshape(-1)


def cholesky_solve(matrix, vector):
    factor = jnp.linalg.cholesky(matrix)
    middle = lax.linalg.triangular_solve(factor, vector[:, None], left_side=True, lower=True)
    answer = lax.linalg.triangular_solve(
        factor, middle, left_side=True, lower=True, transpose_a=True
    )
    return answer[:, 0]


def on_device(template, science, variance, col_taps, row_taps, stamp_rows, stamp_cols):
    tap_count = col_taps.shape[1]
    margin = (tap_count - 1) // 2
    kernels = col_taps.shape[0]
    blocks = kernels // KBLK
    science_map = science[0]
    variance_map = variance[0]
    inverse = 1.0 / variance_map
    gathered = lax.all_gather(template, "visit", axis=0, tiled=True)
    padded_tile = with_halo(gathered, (("sky", 1),), margin)
    image_list = []
    for block_index in range(blocks):
        image_list.append(
            row_pass(
                column_pass(padded_tile, col_taps[block_index * KBLK : (block_index + 1) * KBLK]),
                row_taps[block_index * KBLK : (block_index + 1) * KBLK],
            )
        )
    convolved = jnp.concatenate(image_list, axis=0)
    row_starts = stamp_rows[0, 0]
    col_starts = stamp_cols[0, 0]
    design_core = extract_stamps(convolved, row_starts, col_starts)
    design = jnp.concatenate(
        [design_core, jnp.ones((1, design_core.shape[1]), design_core.dtype)], axis=0
    ).astype(jnp.float32)
    weights = 1.0 / extract_plane(variance_map, row_starts, col_starts)
    values = extract_plane(science_map, row_starts, col_starts)
    partial_normal = jnp.dot(design * weights[None, :], design.T, precision=lax.Precision.HIGHEST)
    partial_target = jnp.dot(design, weights * values, precision=lax.Precision.HIGHEST)
    normal, target = lax.psum((partial_normal, partial_target), "sky")
    solution = cholesky_solve(normal, target)

    def model_step(block_index, total):
        images = lax.dynamic_slice_in_dim(convolved, block_index * KBLK, KBLK, 0).astype(
            jnp.float32
        )
        share = lax.dynamic_slice_in_dim(solution, block_index * KBLK, KBLK, 0)
        return total + jnp.tensordot(share, images, axes=1, precision=lax.Precision.HIGHEST)

    model_map = lax.fori_loop(0, blocks, model_step, jnp.zeros(science_map.shape, jnp.float32))
    residual = science_map - model_map - solution[kernels]
    difference = (residual / jnp.sqrt(variance_map))[None, :, :]
    weighted = residual / variance_map
    numerator, weight_total = (
        lax.psum_scatter(weighted, "visit", scatter_dimension=0, tiled=True),
        lax.psum_scatter(inverse, "visit", scatter_dimension=0, tiled=True),
    )
    detection = numerator / jnp.sqrt(weight_total)
    return (difference, solution[None, :], detection)


def solution(mesh):
    in_specs = (
        P(("group", "visit"), "sky"),
        P(("group", "visit"), None, "sky"),
        P(("group", "visit"), None, "sky"),
        P(),
        P(),
        P(("group", "visit"), "sky", None),
        P(("group", "visit"), "sky", None),
    )
    out_specs = (
        P(("group", "visit"), None, "sky"),
        P(("group", "visit"), None),
        P(("group", "visit"), "sky"),
    )
    return jax.shard_map(
        on_device, mesh=mesh, in_specs=in_specs, out_specs=out_specs, check_vma=False
    )
```

profile of v0, /device:TPU:0, one launch (start us, length us, event | category | flops | bytes accessed | tf_op | source)
XLA Modules:
  0.0 237.8 jit_solution(4948356048800179354)
XLA Ops:
  0.6 23.3 %all-gather = bf16[16,2,128]{2,1,0:T(2,128)(2,1)S(1)} all-gather(bf16[1,2,128]{2,1,0:T(2,128)(2,1)} %bitcast.593), channel_id=1, replica_groups=mesh['group'=2,'visit'=16,'sky'=1] {'visit'}, dimensions={0}, use_global_device_ids=true | all-gather | bytes 8704 | tf_op jit(solution)/shard_map/all_gather | solution.py:110
  28.4 1.8 fusion.33
  30.2 1.7 fusion.32
  32.0 1.8 fusion.31
  33.9 1.8 fusion.30
  35.7 1.8 fusion.29
  37.6 1.9 fusion.28
  39.5 30.6 %while.18 = (s32[]{:T(128)}, f32[32,128]{1,0:T(8,128)S(1)}, s32[16,2]{0,1:T(2,128)S(1)}, f32[16,16,16]{2,1,0:T(8,128)S(1)}, s32[]{:T(128)}) while((s32[]{:T(128)}, f32[32,128]{1,0:T(8,128)S(1)}, s32[16,2]{0,1:T(2,128)S(1)}, f32[16,16,16]{2,1,0:T(8,128)S(1)}, s32[]{:T(128)}) %tuple.319), condition=%wide.while_cond.1, body=%wide.while_body.1.sunk | while | flops 2 | bytes 16493 | solution.py:88
  70.1 31.5 %while.19 = (s32[]{:T(128)}, f32[32,128]{1,0:T(8,128)S(1)}, s32[16,2]{0,1:T(2,128)S(1)}, f32[16,16,16]{2,1,0:T(8,128)S(1)}, s32[]{:T(128)}) while((s32[]{:T(128)}, f32[32,128]{1,0:T(8,128)S(1)}, s32[16,2]{0,1:T(2,128)S(1)}, f32[16,16,16]{2,1,0:T(8,128)S(1)}, s32[]{:T(128)}) %tuple.321), condition=%wide.while_cond.2, body=%wide.while_body.2.sunk | while | flops 2 | bytes 16493 | solution.py:88
  112.6 45.1 %while.17 = (s32[]{:T(128)}, bf16[49,32,128]{2,1,0:T(8,128)(2,1)S(1)}, s32[16,3]{0,1:T(4,128)S(1)}, bf16[16,49,16,16]{3,2,1,0:T(8,128)(2,1)}, s32[]{:T(128)}) while((s32[]{:T(128)}, bf16[49,32,128]{2,1,0:T(8,128)(2,1)S(1)}, s32[16,3]{0,1:T(4,128)S(1)}, bf16[16,49,16,16]{3,2,1,0:T(8,128)(2,1)}, s32[]{:T(128)}) %tuple.312), condition=%wide.while_cond, body=%wide.while_body.sunk | while | flops 2 | bytes 227433 | solution.py:77
  113.3 2.1 bitcast_dynamic-update-slice_fusion.6
  116.1 2.1 bitcast_dynamic-update-slice_fusion.6
  118.9 2.2 bitcast_dynamic-update-slice_fusion.6
  121.8 2.2 bitcast_dynamic-update-slice_fusion.6
  124.6 2.1 bitcast_dynamic-update-slice_fusion.6
  127.4 2.2 bitcast_dynamic-update-slice_fusion.6
  130.2 2.1 bitcast_dynamic-update-slice_fusion.6
  133.0 2.2 bitcast_dynamic-update-slice_fusion.6
  135.9 2.1 bitcast_dynamic-update-slice_fusion.6
  138.7 2.2 bitcast_dynamic-update-slice_fusion.6
  141.5 2.2 bitcast_dynamic-update-slice_fusion.6
  144.3 2.2 bitcast_dynamic-update-slice_fusion.6
  147.1 2.2 bitcast_dynamic-update-slice_fusion.6
  150.0 2.1 bitcast_dynamic-update-slice_fusion.6
  152.8 2.2 bitcast_dynamic-update-slice_fusion.6
  155.6 2.1 bitcast_dynamic-update-slice_fusion.6
  157.7 4.3 %copy.27 = bf16[49,16,16,16]{0,3,2,1:T(8,128)(2,1)S(1)} copy(bf16[49,16,16,16]{3,2,0,1:T(8,128)(2,1)} %bitcast.581) | data formatting | bytes 802816 | tf_op jit(solution)/shard_map/transpose | solution.py:82
  162.1 2.4 %fusion.11 = f32[50,50]{1,0:T(8,128)S(1)} fusion(f32[4096]{0:T(1024)S(1)} %div.38, bf16[49,4096]{0,1:T(8,128)(2,1)S(1)} %bitcast.579), kind=kOutput, calls=%fused_computation.20 | convolution fusion | flops 123289600 | bytes 427792 | tf_op jit(solution)/shard_map/dot_general | solution.py:129
  164.6 4.6 %cholesky.16 = f32[50,50]{1,0:T(8,128)S(1)} custom-call(f32[50,50]{1,0:T(8,128)S(1)} %fusion.511), custom_call_target="Cholesky" | custom-call | tf_op jit(solution)/shard_map/jit(cholesky)/cholesky | solution.py:94
  170.5 3.8 %custom-call.8 = f32[1,50,50]{1,2,0:T(8,128)S(1)} custom-call(f32[1,50,50]{2,1,0:T(8,128)S(1)} %fusion.507), custom_call_target="InvertDiagBlocksLowerTriangular" | custom-call | tf_op jit(solution)/shard_map/triangular_solve | solution.py:96
  175.8 2.3 while.20
  179.5 57.8 %all-reduce.10 = (f32[32,128]{1,0:T(8,128)S(1)}, f32[32,128]{1,0:T(8,128)S(1)}) all-reduce(f32[32,128]{1,0:T(8,128)S(1)} %get-tuple-element.164, f32[32,128]{1,0:T(8,128)S(1)} %get-tuple-element.162), channel_id=3, replica_groups=mesh['group'=2,'visit'=16,'sky'=1] {'visit'}, use_global_device_ids=true, to_apply=%region_5.6.clone | all-reduce | flops 8192 | bytes 65536
  (242 shorter events, 93.8 us)
Async XLA Ops:
  0.6 31.4 %copy-start.5 = (bf16[49,31]{0,1:T(8,128)(2,1)S(1)}, bf16[49,31]{0,1:T(8,128)(2,1)}, u32[]{:S(2)}) copy-start(bf16[49,31]{0,1:T(8,128)(2,1)} %param.12) | copy-start | bytes 9118
  24.0 79.1 %collective-permute-start = (bf16[32,15]{1,0:T(8,128)(2,1)S(1)}, bf16[32,15]{1,0:T(8,128)(2,1)S(1)}, u32[]{:S(2)}, u32[]{:S(2)}) collective-permute-start(bf16[32,15]{1,0:T(8,128)(2,1)S(1)} %get-tuple-element.389), channel_id=1, source_target_pairs={} | collective-permute-start | bytes 2888 | tf_op jit(solution)/shard_map/ppermute | solution.py:18
  24.6 78.5 %collective-permute-start.1 = (bf16[32,15]{1,0:T(8,128)(2,1)S(1)}, bf16[32,15]{1,0:T(8,128)(2,1)S(1)}, u32[]{:S(2)}, u32[]{:S(2)}) collective-permute-start(bf16[32,15]{1,0:T(8,128)(2,1)S(1)} %get-tuple-element.390), channel_id=1, source_target_pairs={} | collective-permute-start | bytes 2888 | tf_op jit(solution)/shard_map/ppermute | solution.py:20
  28.4 11.0 %copy-start.3 = (s32[1,1,16]{2,1,0:T(1,128)S(1)}, s32[1,1,16]{2,1,0:T(1,128)}, u32[]{:S(2)}) copy-start(s32[1,1,16]{2,1,0:T(1,128)} %param.15) | copy-start | bytes 196
  28.4 11.0 %copy-start.4 = (s32[1,1,16]{2,1,0:T(1,128)S(1)}, s32[1,1,16]{2,1,0:T(1,128)}, u32[]{:S(2)}) copy-start(s32[1,1,16]{2,1,0:T(1,128)} %param.14) | copy-start | bytes 196
  30.2 9.3 %copy-start = (f32[1,32,128]{2,1,0:T(8,128)S(1)}, f32[1,32,128]{2,1,0:T(8,128)}, u32[]{:S(2)}) copy-start(f32[1,32,128]{2,1,0:T(8,128)} %param.11) | copy-start | bytes 49156
  30.2 39.9 %copy-start.1 = (f32[1,32,128]{2,1,0:T(8,128)S(1)}, f32[1,32,128]{2,1,0:T(8,128)}, u32[]{:S(2)}) copy-start(f32[1,32,128]{2,1,0:T(8,128)} %param.10) | copy-start | bytes 49156
  32.0 69.9 %copy-start.6 = (u32[32]{0:T(128)S(1)}, u32[32]{0:T(128)}, u32[]{:S(2)}) copy-start(u32[32]{0:T(128)} %constant.223) | copy-start | bytes 388
  103.1 4.8 %copy-start.7 = (bf16[7,158,128]{1,0,2:T(8,128)(2,1)S(1)}, bf16[7,158,128]{1,0,2:T(8,128)(2,1)}, u32[]{:S(2)}) copy-start(bf16[7,158,128]{1,0,2:T(8,128)(2,1)} %fusion.28) | copy-start | bytes 849412
  178.2 59.7 %copy-start.2 = (f32[50]{0:T(128)}, f32[50]{0:T(128)S(1)}, u32[]{:S(2)}) copy-start(f32[50]{0:T(128)S(1)} %get-tuple-element.611) | copy-start | bytes 604
where the time goes:
time: 239 us; the launch traced here: 238 us
  local copies, waits for them, and re-layouts  113 us (47%)
  blocking collectives  81.1 us (34%)
  matrix products  27 us (11%)
  other arithmetic  13 us (5%)
    gather x144, local copies, waits for them, and re-layouts  107 us
    unnamed x1, blocking collectives  57.8 us
    all_gather x1, blocking collectives, on_device(): gathered = lax.all_gather(template, 'visit', axis=0, tiled=True)  23.3 us
    dot_general x7, matrix products, column_pass(): jnp.einsum('kj,jci->kic', taps_block.astype(jnp.float32), selectors)  12.6 us
    another operation x3, other arithmetic, cholesky_solve(): factor = jnp.linalg.cholesky(matrix)  5.24 us
    dot_general x7, matrix products, column_pass(): jnp.einsum('ri,kic->krc', padded, band_mats, preferred_element_type=jnp.f...  4.89 us
  transfers between devices with their start and end apart: 2, of which 0 were waited for; matrix products, arithmetic and copies ran while one was open for 32% of the time, Pallas kernels for 0%

commit v1 on v0

v1 whole, which is shorter than its diff:
```python
import jax
import jax.numpy as jnp
from jax import lax
from jax.experimental import pallas as pl
from jax.experimental.pallas import tpu as pltpu
from jax.sharding import PartitionSpec as P

STAMP = 16
SUB = 8
LANE = 128
UNROLL = 32
F32 = jnp.float32
BF16 = jnp.bfloat16


def ceil_to(value, step):
    return (value + step - 1) // step * step


def each(count, body):
    if count <= UNROLL:
        for index in range(count):
            body(index)
    else:
        lax.fori_loop(0, count, lambda index, carry: (body(index), carry)[1], 0)


def lanes_of(index, width):
    if isinstance(index, int):
        return slice(index * width, (index + 1) * width)
    return pl.ds(pl.multiple_of(index * width, width), width)


def split_bf16(value, pieces):
    out = []
    for piece in range(pieces):
        part = value.astype(BF16)
        out.append(part)
        if piece + 1 < pieces:
            value = value - part.astype(F32)
    return out


def load_taps(taps_ref, pad_ref):
    kernels, taps = taps_ref.shape
    pad_ref[...] = jnp.zeros(pad_ref.shape, F32)
    pad_ref[0:kernels, 0:taps] = taps_ref[...].astype(F32)


def column_stage(tmpl_ref, edge_ref, col_taps_ref, pad_ref, cols_ref, tap_count):
    height, width = tmpl_ref.shape
    margin = (tap_count - 1) // 2
    span = ceil_to(tap_count, SUB)
    load_taps(col_taps_ref, pad_ref)
    flip = (
        lax.broadcasted_iota(jnp.int32, (span, span), 0)
        + lax.broadcasted_iota(jnp.int32, (span, span), 1)
        == tap_count - 1
    ).astype(BF16)
    taps = jnp.dot(
        pad_ref[:, 0:span].astype(BF16), flip, preferred_element_type=F32
    ).astype(BF16)
    place = lax.broadcasted_iota(jnp.int32, (span, width), 1) + (
        margin - lax.broadcasted_iota(jnp.int32, (span, width), 0)
    )
    inside = (place >= 0) & (place < width)
    groups = cols_ref.shape[1]

    def shifted(row):
        line = jnp.broadcast_to(tmpl_ref[pl.ds(row, 1), :], (span, width))
        line = pltpu.roll(line, width - margin, 1, stride=1, stride_axis=0)
        if edge_ref is None:
            return jnp.where(inside, line, 0.0).astype(BF16)
        side = jnp.broadcast_to(edge_ref[pl.ds(row, 1), :], (span, width))
        side = pltpu.roll(side, width - margin, 1, stride=1, stride_axis=0)
        return jnp.where(inside, line, side).astype(BF16)

    def pair(index):
        both = jnp.concatenate([shifted(2 * index), shifted(2 * index + 1)], axis=1)
        result = jnp.dot(taps, both, preferred_element_type=F32)
        result = result.astype(BF16).astype(F32)
        for half in range(2):
            for group in range(groups):
                cols_ref[2 * index + half + margin, group] = result[
                    SUB * group : SUB * (group + 1), width * half : width * (half + 1)
                ]

    each(height // 2, pair)


def row_stage(row_taps_ref, pad_ref, spread_ref, cols_ref, conv_ref, kernels, tap_count):
    height, groups, _, width = conv_ref.shape
    margin = (tap_count - 1) // 2
    load_taps(row_taps_ref, pad_ref)
    for tap in range(tap_count):
        column = jnp.broadcast_to(
            pad_ref[0 : groups * SUB, tap : tap + 1], (groups * SUB, width)
        )
        for group in range(groups):
            spread_ref[group, tap] = column[SUB * group : SUB * (group + 1)]
    static = height <= UNROLL
    if not static:
        edge = jnp.zeros((margin, groups, SUB, width), F32)
        cols_ref[0:margin] = edge
        cols_ref[height + margin : height + 2 * margin] = edge
    block = 8

    def group_body(group, first):
        acc = [None] * block
        for step in range(block + 2 * margin):
            if static and not 0 <= first + step - margin < height:
                continue
            value = cols_ref[first + step, group]
            for out in range(block):
                tap = step - out
                if 0 <= tap < tap_count:
                    term = spread_ref[group, tap] * value
                    acc[out] = term if acc[out] is None else acc[out] + term
        ones = (
            lax.broadcasted_iota(jnp.int32, (SUB, width), 0) + SUB * group == kernels
        )
        for out in range(block):
            rounded = acc[out].astype(BF16).astype(F32)
            conv_ref[first + out, group] = jnp.where(ones, 1.0, rounded)

    def loop_groups(first):
        lax.fori_loop(0, groups, lambda g, c: (group_body(g, first), c)[1], 0)

    if static:
        for first in range(0, height, block):
            loop_groups(first)
    else:
        lax.fori_loop(
            0, height // block, lambda b, c: (loop_groups(b * block), c)[1], 0
        )


def weight_stage(var_ref, rows_ref, cols_ref, weight_ref, inverse_ref):
    height, width = weight_ref.shape
    stamps = rows_ref.shape[-1]

    def block(index):
        first = index * SUB
        row = lax.broadcasted_iota(jnp.int32, (SUB, width), 0) + first
        col = lax.broadcasted_iota(jnp.int32, (SUB, width), 1)
        count = jnp.zeros((SUB, width), F32)
        for stamp in range(stamps):
            down = row - rows_ref[0, 0, stamp]
            along = col - cols_ref[0, 0, stamp]
            held = (down >= 0) & (down < STAMP) & (along >= 0) & (along < STAMP)
            count = count + jnp.where(held, 1.0, 0.0)
        if not isinstance(first, int):
            first = pl.multiple_of(first, SUB)
        inverse = 1.0 / var_ref[0, pl.ds(first, SUB), :]
        inverse_ref[pl.ds(first, SUB), :] = inverse
        weight_ref[pl.ds(first, SUB), :] = inverse * count

    each(height // SUB, block)


def normal_stage(sci_ref, weight_ref, conv_ref, left_ref, right_ref, kernels):
    height, groups, _, width = conv_ref.shape
    size = right_ref.shape[0]
    tall = groups * SUB
    line = lax.broadcasted_iota(jnp.int32, (size, width), 0)

    def one(row):
        design = conv_ref[row].reshape(tall, width)
        if size > tall:
            design = jnp.concatenate([design, jnp.zeros((size - tall, width), F32)], axis=0)
        weight = jnp.broadcast_to(weight_ref[pl.ds(row, 1), :], (size, width))
        science = jnp.broadcast_to(sci_ref[0, pl.ds(row, 1), :], (size, width))
        high, low = split_bf16(design * weight, 2)
        where = lanes_of(row, width)
        left_ref[0:size, where] = high
        left_ref[size : 2 * size, where] = low
        full = design
        for index, part in enumerate(split_bf16(science, 3)):
            full = jnp.where(line == kernels + 1 + index, part.astype(F32), full)
        right_ref[:, where] = full.astype(BF16)

    each(height, one)
    product = lax.dot_general(
        left_ref[...],
        right_ref[...],
        (((1,), (1,)), ((), ())),
        preferred_element_type=F32,
    )
    return product[0:size] + product[size : 2 * size]


def solve_stage(normal, kernels):
    unknowns = kernels + 1
    width = LANE
    groups = ceil_to(unknowns, SUB) // SUB
    size = normal.shape[1]
    parts = [normal[SUB * g : SUB * (g + 1)] for g in range(groups)]
    if size < width:
        parts = [
            jnp.concatenate([part, jnp.zeros((SUB, width - size), F32)], axis=1)
            for part in parts
        ]

    def lane(value, index):
        return jnp.broadcast_to(value[:, index : index + 1], (SUB, width))

    def sub(value, index):
        return jnp.broadcast_to(value[index : index + 1, :], (SUB, width))

    total = [
        lane(p, unknowns) + (lane(p, unknowns + 1) + lane(p, unknowns + 2)) for p in parts
    ]
    column = lax.broadcasted_iota(jnp.int32, (SUB, width), 1)
    row = lax.broadcasted_iota(jnp.int32, (SUB, width), 0)
    parts = [jnp.where(column == unknowns, t, p) for p, t in zip(parts, total)]
    step = 0
    while step < unknowns:
        if step + 1 < unknowns:
            first, second = step, step + 1
            g0, s0, g1, s1 = first // SUB, first % SUB, second // SUB, second % SUB
            c0 = [lane(p, first) for p in parts]
            c1 = [lane(p, second) for p in parts]
            r0, r1 = sub(parts[g0], s0), sub(parts[g1], s1)
            a, b = sub(c0[g0], s0), sub(c1[g0], s0)
            e, d = sub(c0[g1], s1), sub(c1[g1], s1)
            inverse = 1.0 / (a * d - b * e)
            q0 = (d * inverse) * r0 - (b * inverse) * r1
            q1 = (a * inverse) * r1 - (e * inverse) * r0
            parts = [p - x * q0 - y * q1 for p, x, y in zip(parts, c0, c1)]
            parts[g0] = jnp.where(row == s0, q0, parts[g0])
            parts[g1] = jnp.where(row == s1, q1, parts[g1])
            step += 2
        else:
            g0, s0 = step // SUB, step % SUB
            c0 = [lane(p, step) for p in parts]
            q0 = sub(parts[g0], s0) * (1.0 / sub(c0[g0], s0))
            parts = [p - x * q0 for p, x in zip(parts, c0)]
            parts[g0] = jnp.where(row == s0, q0, parts[g0])
            step += 1
    values = [lane(p, unknowns) for p in parts]
    last = [jnp.where(row + SUB * g < unknowns, v, 0.0) for g, v in enumerate(values)]
    return last


def residual_stage(values, conv_ref, sci_ref, var_ref, inverse_ref, diff_ref, out_ref, rows_each):
    height, groups, _, width = conv_ref.shape

    def block(index):
        first = index * SUB
        if not isinstance(first, int):
            first = pl.multiple_of(first, SUB)
        lines = []
        for row in range(SUB):
            total = conv_ref[first + row, 0] * values[0]
            for group in range(1, groups):
                total = total + conv_ref[first + row, group] * values[group]
            lines.append(jnp.sum(total, axis=0, keepdims=True))
        model = jnp.concatenate(lines, axis=0)
        here = pl.ds(first, SUB)
        residual = sci_ref[0, here, :] - model
        diff_ref[0, here, :] = residual / jnp.sqrt(var_ref[0, here, :])
        inverse = inverse_ref[here, :]
        weighted = residual * inverse
        for start in range(0, SUB, rows_each):
            target = (first + start) // rows_each
            out_ref[target, 0:rows_each, :] = weighted[start : start + rows_each]
            out_ref[target, rows_each : 2 * rows_each, :] = inverse[start : start + rows_each]

    each(height // SUB, block)


def store_coefficients(values, coef_ref, unknowns):
    row = lax.broadcasted_iota(jnp.int32, (SUB, LANE), 0)
    column = lax.broadcasted_iota(jnp.int32, (SUB, LANE), 1)
    total = jnp.zeros((SUB, LANE), F32)
    for group, value in enumerate(values):
        total = total + jnp.where(column == row + SUB * group, value, 0.0)
    coef_ref[...] = jnp.sum(total, axis=0, keepdims=True)[:, 0:unknowns]


def fit(template, edge, science, variance, col_taps, row_taps, stamp_rows, stamp_cols, rows_each, sky):
    height, width = template.shape
    kernels, tap_count = col_taps.shape
    unknowns = kernels + 1
    margin = (tap_count - 1) // 2
    groups = ceil_to(unknowns, SUB) // SUB
    size = ceil_to(unknowns + 3, 2 * SUB)
    whole = sky == 1
    vmem = pl.BlockSpec(memory_space=pltpu.VMEM)
    smem = pl.BlockSpec(memory_space=pltpu.SMEM)
    scratch = [
        pltpu.VMEM((ceil_to(kernels, 2 * SUB), LANE), F32),
        pltpu.VMEM((height + 2 * margin, groups, SUB, width), F32),
        pltpu.VMEM((groups, tap_count, SUB, width), F32),
        pltpu.VMEM((height, width), F32),
        pltpu.VMEM((height, width), F32),
        pltpu.VMEM((2 * size, height * width), BF16),
        pltpu.VMEM((size, height * width), BF16),
    ]
    conv_shape = (height, groups, SUB, width)
    out_shapes = [
        jax.ShapeDtypeStruct((1, height, width), F32),
        jax.ShapeDtypeStruct((1, unknowns), F32),
        jax.ShapeDtypeStruct((height // rows_each, 2 * rows_each, width), F32),
    ]
    params = pltpu.CompilerParams(vmem_limit_bytes=60 * 1024 * 1024)

    def front(tmpl_ref, edge_ref, sci_ref, var_ref, ct_ref, rt_ref, sr_ref, sc_ref, conv_ref, tmp):
        pad, cols, spread, weight, inverse, left, right = tmp
        column_stage(tmpl_ref, edge_ref, ct_ref, pad, cols, tap_count)
        row_stage(rt_ref, pad, spread, cols, conv_ref, kernels, tap_count)
        weight_stage(var_ref, sr_ref, sc_ref, weight, inverse)
        return normal_stage(sci_ref, weight, conv_ref, left, right, kernels)

    def back(normal, conv_ref, sci_ref, var_ref, inverse, diff_ref, coef_ref, out_ref):
        values = solve_stage(normal, kernels)
        store_coefficients(values, coef_ref, unknowns)
        residual_stage(values, conv_ref, sci_ref, var_ref, inverse, diff_ref, out_ref, rows_each)

    if whole:

        def kernel(tmpl, sci, var, ct, rt, sr, sc, diff, coef, out, conv, *tmp):
            normal = front(tmpl, None, sci, var, ct, rt, sr, sc, conv, tmp)
            back(normal, conv, sci, var, tmp[4], diff, coef, out)

        return pl.pallas_call(
            kernel,
            out_shape=out_shapes,
            in_specs=[vmem] * 5 + [smem] * 2,
            out_specs=[vmem] * 3,
            scratch_shapes=[pltpu.VMEM(conv_shape, F32)] + scratch,
            compiler_params=params,
        )(template, science, variance, col_taps, row_taps, stamp_rows, stamp_cols)

    def first(tmpl, edges, sci, var, ct, rt, sr, sc, conv, inv, normal, *tmp):
        normal[...] = front(tmpl, edges, sci, var, ct, rt, sr, sc, conv, tmp)
        inv[...] = tmp[4][...]

    conv, inverse, normal = pl.pallas_call(
        first,
        out_shape=[
            jax.ShapeDtypeStruct(conv_shape, F32),
            jax.ShapeDtypeStruct((height, width), F32),
            jax.ShapeDtypeStruct((size, size), F32),
        ],
        in_specs=[vmem] * 6 + [smem] * 2,
        out_specs=[vmem] * 3,
        scratch_shapes=scratch,
        compiler_params=params,
    )(template, edge, science, variance, col_taps, row_taps, stamp_rows, stamp_cols)
    normal = lax.psum(normal, "sky")

    def second(normal, conv, sci, var, inv, diff, coef, out):
        back(normal[...], conv, sci, var, inv, diff, coef, out)

    return pl.pallas_call(
        second,
        out_shape=out_shapes,
        in_specs=[vmem] * 5,
        out_specs=[vmem] * 3,
        compiler_params=params,
    )(normal, conv, science, variance, inverse)


def sky_edges(tile, margin, sky):
    ends = sky - 1
    width = tile.shape[1]
    head = tile[:, 0:margin]
    tail = tile[:, width - margin :]
    after = lax.ppermute(head, "sky", [(i + 1, i) for i in range(ends)])
    before = lax.ppermute(tail, "sky", [(i, i + 1) for i in range(ends)])
    middle = jnp.zeros((tile.shape[0], width - 2 * margin), tile.dtype)
    return jnp.concatenate([after, middle, before], axis=1)


def solution(mesh):
    visits = mesh.shape["visit"]
    sky = mesh.shape["sky"]

    def on_device(template, science, variance, col_taps, row_taps, stamp_rows, stamp_cols):
        rows_each, width = template.shape
        margin = (col_taps.shape[1] - 1) // 2
        copies = jnp.broadcast_to(template.astype(F32)[None], (visits, rows_each, width))
        tile = lax.all_to_all(copies, "visit", 0, 0, tiled=True).reshape(-1, width)
        edge = sky_edges(tile, margin, sky) if sky > 1 else None
        difference, coefficients, shares = fit(
            tile, edge, science, variance, col_taps, row_taps, stamp_rows, stamp_cols, rows_each, sky
        )
        shares = lax.all_to_all(shares, "visit", 0, 0, tiled=True)
        total = jnp.sum(shares, axis=0)
        detection = total[0:rows_each] / jnp.sqrt(total[rows_each:])
        return difference, coefficients, detection

    in_specs = (
        P(("group", "visit"), "sky"),
        P(("group", "visit"), None, "sky"),
        P(("group", "visit"), None, "sky"),
        P(),
        P(),
        P(("group", "visit"), "sky", None),
        P(("group", "visit"), "sky", None),
    )
    out_specs = (
        P(("group", "visit"), None, "sky"),
        P(("group", "visit"), None),
        P(("group", "visit"), "sky"),
    )
    return jax.shard_map(
        on_device, mesh=mesh, in_specs=in_specs, out_specs=out_specs, check_vma=False
    )
```

time: 239 us -> 36.1 us (0.15)
  local copies, waits for them, and re-layouts: 113 us -> 3.28 us
  blocking collectives: 81.1 us -> 10.1 us
  matrix products: 27 us -> 0 us
  other arithmetic: 13 us -> 0.6 us
  Pallas kernels: 0 us -> 8.59 us
  starting transfers between devices: 1.3 us -> 7.52 us
  waiting for transfers between devices: 0.01 us -> 5.07 us
    gather x144 -> x0, local copies, waits for them, and re-layouts: 107 us -> none
    unnamed x1 -> x0, blocking collectives: 57.8 us -> none
    dot_general x30 -> x0, matrix products: 26.7 us -> none  [the longest x7 12.6 us: column_pass(): jnp.einsum('kj,jci->kic', taps_block.astype(jnp.float32), selectors)]
    all_gather x1 -> x0, blocking collectives: 23.3 us -> none  [on_device(): gathered = lax.all_gather(template, 'visit', axis=0, tiled=True)]
    all_to_all x0 -> x1, blocking collectives: none -> 10.1 us  [on_device(): shares = lax.all_to_all(shares, 'visit', 0, 0, tiled=True)]
    another operation x5 -> x0, other arithmetic: 9.72 us -> none  [the longest x3 5.24 us: cholesky_solve(): factor = jnp.linalg.cholesky(matrix)]
    pallas_call x0 -> x1, Pallas kernels: none -> 8.59 us  [fit(): pl.pallas_call(kernel, out_shape=out_shapes, in_specs=[vmem] * 5 + [smem]...]
    all_to_all x0 -> x1, starting transfers between devices: none -> 7.52 us  [on_device(): tile = lax.all_to_all(copies, 'visit', 0, 0, tiled=True).reshape(-1, width)]
  transfers between devices with their start and end apart: 2 -> 1, of which waited for: 0 -> 1; matrix products, arithmetic and copies ran while one was open for 32% -> 4% of each run, Pallas kernels for 0% -> 0%
where the time goes in v1:
time: 36.1 us; the launch traced here: 35.8 us
  blocking collectives  10.1 us (28%)
  Pallas kernels  8.59 us (24%)
  starting transfers between devices  7.52 us (21%)
  waiting for transfers between devices  5.07 us (14%)
  local copies, waits for them, and re-layouts  3.28 us (9%)
  between operations  0.66 us (2%)
  other arithmetic  0.6 us (2%)
    all_to_all x1, blocking collectives, on_device(): shares = lax.all_to_all(shares, 'visit', 0, 0, tiled=True)  10.1 us
    pallas_call x1, Pallas kernels, fit(): pl.pallas_call(kernel, out_shape=out_shapes, in_specs=[vmem] * 5 + [smem]...  8.59 us
    all_to_all x1, starting transfers between devices, on_device(): tile = lax.all_to_all(copies, 'visit', 0, 0, tiled=True).reshape(-1, width)  7.52 us
    all_to_all x1, waiting for transfers between devices, on_device(): tile = lax.all_to_all(copies, 'visit', 0, 0, tiled=True).reshape(-1, width)  5.07 us
    unnamed x8, local copies, waits for them, and re-layouts  2.02 us
    broadcast_in_dim x1, local copies, waits for them, and re-layouts, on_device(): jnp.broadcast_to(template.astype(F32)[None], (visits, rows_each, width))  1.27 us
  transfers between devices with their start and end apart: 1, of which 1 were waited for; matrix products, arithmetic and copies ran while one was open for 4% of the time, Pallas kernels for 0%

profile of v1, /device:TPU:0, one launch (start us, length us, event | category | flops | bytes accessed | tf_op | source)
XLA Modules:
  0.0 35.8 jit_solution(12659070803643003934)
XLA Ops:
  0.6 1.3 %broadcast_in_dim.2 = f32[16,2,128]{2,1,0:T(2,128)} broadcast(bf16[2,128]{1,0:T(2,128)(2,1)} %param.7), dimensions={1,2} | broadcast | bytes 16896 | tf_op jit(solution)/shard_map/broadcast_in_dim | solution.py:383
  1.9 0.0 copy-start.1
  1.9 7.5 %all-to-all-start = ((f32[16,2,128]{2,1,0:T(2,128)}), f32[16,2,128]{2,1,0:T(2,128)S(1)}, u32[]{:S(2)}, u32[]{:S(2)}) async-start(f32[16,2,128]{2,1,0:T(2,128)} %broadcast_in_dim.2), calls=%async_computation | async-start | bytes 32768 | tf_op jit(solution)/shard_map/all_to_all | solution.py:384
  9.4 0.0 copy-done.1
  9.4 0.0 copy-start.2
  9.4 0.7 %copy.10.ct = bf16[49,31]{1,0:T(8,128)(2,1)} copy(bf16[49,31]{0,1:T(8,128)(2,1)S(1)} %copy-done.1) | data formatting | bytes 6076 | tf_op args[3]
  10.2 0.0 copy-done.2
  10.2 0.7 %copy.11.rt = bf16[49,31]{1,0:T(8,128)(2,1)} copy(bf16[49,31]{0,1:T(8,128)(2,1)S(1)} %copy-done.2) | data formatting | bytes 6076 | tf_op args[4]
  10.9 5.1 %all-to-all-done = f32[16,2,128]{2,1,0:T(2,128)S(1)} async-done(((f32[16,2,128]{2,1,0:T(2,128)}), f32[16,2,128]{2,1,0:T(2,128)S(1)}, u32[]{:S(2)}, u32[]{:S(2)}) %all-to-all-start) | async-done | bytes 16416 | tf_op jit(solution)/shard_map/all_to_all | solution.py:384
  15.9 0.0 copy-start
  15.9 0.6 %copy-done = f32[16,2,128]{2,1,0:T(2,128)} copy-done((f32[16,2,128]{2,1,0:T(2,128)}, f32[16,2,128]{2,1,0:T(2,128)S(1)}, u32[]{:S(2)}) %copy-start) | copy-done | bytes 16408
  16.5 8.6 %shard_map.94 = (f32[1,32,128]{2,1,0:T(8,128)}, f32[1,50]{1,0:T(1,128)}, f32[16,4,128]{2,1,0:T(4,128)}) custom-call(f32[32,128]{1,0:T(8,128)} %bitcast.1, f32[1,32,128]{2,1,0:T(8,128)} %sci.1, f32[1,32,128]{2,1,0:T(8,128)} %var.1, bf16[49,31]{1,0:T(8,128)(2,1)} %copy.10.ct, bf16[49,31]{1,0:T(8,128)(2,1)} %copy.11.rt, s32[1,1,16]{2,1,0:T(1,128)} %sr.1, ...), custom_call_target="tpu_custom_call" | custom-call | tf_op jit(solution)/shard_map/pallas_call | solution.py:326
  25.1 10.1 %all_to_all.10 = f32[16,4,128]{2,1,0:T(4,128)S(1)} all-to-all(f32[16,4,128]{2,1,0:T(4,128)} %get-tuple-element.8), channel_id=1, replica_groups=mesh['group'=2,'visit'=16,'sky'=1] {'visit'}, dimensions={0} | all-to-all | bytes 65536 | tf_op jit(solution)/shard_map/all_to_all | solution.py:389
  35.2 0.6 %rsqrt_multiply_fusion = f32[2,128]{1,0:T(2,128)} fusion(f32[4,128]{1,0:T(4,128)S(1)} %reduce_sum.9), kind=kLoop, calls=%fused_computation | loop fusion | flops 256 | bytes 3072 | tf_op jit(solution)/shard_map/div | solution.py:391
  (1 shorter events, 0.0 us)
Async XLA Ops:
  1.9 7.5 %copy-start.1 = (bf16[49,31]{0,1:T(8,128)(2,1)S(1)}, bf16[49,31]{0,1:T(8,128)(2,1)}, u32[]{:S(2)}) copy-start(bf16[49,31]{0,1:T(8,128)(2,1)} %param.10) | copy-start | bytes 9118
  1.9 14.0 %all-to-all-start = ((f32[16,2,128]{2,1,0:T(2,128)}), f32[16,2,128]{2,1,0:T(2,128)S(1)}, u32[]{:S(2)}, u32[]{:S(2)}) async-start(f32[16,2,128]{2,1,0:T(2,128)} %broadcast_in_dim.2), calls=%async_computation | async-start | bytes 32768 | tf_op jit(solution)/shard_map/all_to_all | solution.py:384
  9.4 0.7 %copy-start.2 = (bf16[49,31]{0,1:T(8,128)(2,1)S(1)}, bf16[49,31]{0,1:T(8,128)(2,1)}, u32[]{:S(2)}) copy-start(bf16[49,31]{0,1:T(8,128)(2,1)} %param.11) | copy-start | bytes 9118
  15.9 0.6 %copy-start = (f32[16,2,128]{2,1,0:T(2,128)}, f32[16,2,128]{2,1,0:T(2,128)S(1)}, u32[]{:S(2)}) copy-start(f32[16,2,128]{2,1,0:T(2,128)S(1)} %all-to-all-done) | copy-start | bytes 49156

commit v2 on v1

v2 whole, which is shorter than its diff:
```python
import jax
import jax.numpy as jnp
from jax import lax
from jax.experimental import pallas as pl
from jax.experimental.pallas import tpu as pltpu
from jax.sharding import PartitionSpec as P

STAMP = 16
SUB = 8
LANE = 128
UNROLL = 32
CHUNK = 32
F32 = jnp.float32
BF16 = jnp.bfloat16


def ceil_to(value, step):
    return (value + step - 1) // step * step


def each(count, body):
    if count <= UNROLL:
        for index in range(count):
            body(index)
    else:
        lax.fori_loop(0, count, lambda index, carry: (body(index), carry)[1], 0)


def lanes_of(index, width):
    if isinstance(index, int):
        return slice(index * width, (index + 1) * width)
    return pl.ds(pl.multiple_of(index * width, width), width)


def split_bf16(value, pieces):
    out = []
    for piece in range(pieces):
        part = value.astype(BF16)
        out.append(part)
        if piece + 1 < pieces:
            value = value - part.astype(F32)
    return out


def load_taps(taps_ref, pad_ref):
    kernels, taps = taps_ref.shape
    pad_ref[...] = jnp.zeros(pad_ref.shape, F32)
    pad_ref[0:kernels, 0:taps] = taps_ref[...].astype(F32)


def chunk_rows(height):
    rows = min(CHUNK, height)
    return rows, (0 if rows == height else CHUNK // 2)


def taps_stage(col_taps_ref, row_taps_ref, pad_ref, flipped_ref, band_ref, height):
    tap_count = col_taps_ref.shape[1]
    margin = (tap_count - 1) // 2
    span = ceil_to(tap_count, SUB)
    groups = band_ref.shape[0]
    rows, side = chunk_rows(height)
    wide = SUB * (rows + 2 * side)
    load_taps(col_taps_ref, pad_ref)
    flip = (
        lax.broadcasted_iota(jnp.int32, (span, span), 0)
        + lax.broadcasted_iota(jnp.int32, (span, span), 1)
        == tap_count - 1
    ).astype(BF16)
    flipped_ref[...] = jnp.dot(
        pad_ref[:, 0:span].astype(BF16), flip, preferred_element_type=F32
    ).astype(BF16)
    load_taps(row_taps_ref, pad_ref)
    repeat = (
        lax.broadcasted_iota(jnp.int32, (span, wide), 1) // SUB
        == lax.broadcasted_iota(jnp.int32, (span, wide), 0)
    ).astype(BF16)
    spread = jnp.dot(
        pad_ref[0 : groups * SUB, 0:span].astype(BF16), repeat, preferred_element_type=F32
    )
    tall = groups * SUB
    lane = lax.broadcasted_iota(jnp.int32, (tall, wide), 1)
    own = lane % SUB == lax.broadcasted_iota(jnp.int32, (tall, wide), 0) % SUB
    spread = jnp.where(own, spread, 0.0)
    place = lane // SUB - side

    def line(row):
        moved = pltpu.roll(spread, (SUB * (row - margin + side)) % wide, 1)
        return jnp.where((place >= row - margin) & (place <= row + margin), moved, 0.0)

    for row in range(0, rows, 2):
        first, second = line(row), line(row + 1)
        for group in range(groups):
            here = slice(SUB * group, SUB * (group + 1))
            both = jnp.concatenate([first[here], second[here]], axis=0)
            band_ref[group, SUB * row : SUB * (row + 2), :] = both.astype(BF16)


def column_stage(tmpl_ref, edge_ref, flipped_ref, cols_ref, height, tap_count):
    width = tmpl_ref.shape[1]
    margin = (tap_count - 1) // 2
    span = ceil_to(tap_count, SUB)
    groups = cols_ref.shape[0]
    _, side = chunk_rows(height)
    taps = flipped_ref[...]
    place = lax.broadcasted_iota(jnp.int32, (span, width), 1) + (
        margin - lax.broadcasted_iota(jnp.int32, (span, width), 0)
    )
    inside = (place >= 0) & (place < width)
    if side:
        nothing = jnp.zeros((groups, SUB * side, width), BF16)
        cols_ref[:, 0 : SUB * side, :] = nothing
        cols_ref[:, SUB * (side + height) :, :] = nothing

    def shifted(row):
        line = jnp.broadcast_to(tmpl_ref[pl.ds(row, 1), :].astype(F32), (span, width))
        line = pltpu.roll(line, width - margin, 1, stride=1, stride_axis=0)
        if edge_ref is None:
            return jnp.where(inside, line, 0.0).astype(BF16)
        other = jnp.broadcast_to(edge_ref[pl.ds(row, 1), :].astype(F32), (span, width))
        other = pltpu.roll(other, width - margin, 1, stride=1, stride_axis=0)
        return jnp.where(inside, line, other).astype(BF16)

    def pair(index):
        both = jnp.concatenate([shifted(2 * index), shifted(2 * index + 1)], axis=1)
        result = jnp.dot(taps, both, preferred_element_type=F32)
        start = SUB * (2 * index + side)
        if not isinstance(start, int):
            start = pl.multiple_of(start, 2 * SUB)
        for group in range(groups):
            here = result[SUB * group : SUB * (group + 1)]
            two = jnp.concatenate([here[:, 0:width], here[:, width:]], axis=0)
            cols_ref[group, pl.ds(start, 2 * SUB), :] = two.astype(BF16)

    each(height // 2, pair)


def row_stage(band_ref, cols_ref, tail_ref, conv_ref):
    height, groups, _, width = conv_ref.shape
    rows, side = chunk_rows(height)

    def chunk(index):
        first = index * rows
        start = SUB * first
        if not isinstance(start, int):
            start = pl.multiple_of(start, SUB * rows)
        for group in range(groups):
            result = jnp.dot(
                band_ref[group],
                cols_ref[group, pl.ds(start, SUB * (rows + 2 * side)), :],
                preferred_element_type=F32,
            )
            for row in range(rows):
                value = result[SUB * row : SUB * (row + 1)].astype(BF16).astype(F32)
                if group == groups - 1:
                    value = value + tail_ref[first + row]
                conv_ref[first + row, group] = value

    each(height // rows, chunk)


def weight_stage(sci_ref, var_ref, rows_ref, cols_ref, weight_ref, inverse_ref, tail_ref, kernels):
    height, width = weight_ref.shape
    stamps = rows_ref.shape[-1]
    sub = lax.broadcasted_iota(jnp.int32, (SUB, width), 0)
    col = lax.broadcasted_iota(jnp.int32, (SUB, width), 1)
    ones = kernels % SUB

    def block(index):
        first = index * SUB
        row = sub + first
        count = jnp.zeros((SUB, width), F32)
        for stamp in range(stamps):
            down = row - rows_ref[0, 0, stamp]
            along = col - cols_ref[0, 0, stamp]
            held = (down >= 0) & (down < STAMP) & (along >= 0) & (along < STAMP)
            count = count + jnp.where(held, 1.0, 0.0)
        if not isinstance(first, int):
            first = pl.multiple_of(first, SUB)
        inverse = 1.0 / var_ref[0, pl.ds(first, SUB), :]
        inverse_ref[pl.ds(first, SUB), :] = inverse
        weight_ref[pl.ds(first, SUB), :] = inverse * count
        pieces = [p.astype(F32) for p in split_bf16(sci_ref[0, pl.ds(first, SUB), :], 3)]
        for line in range(SUB):
            value = jnp.where(sub == ones, 1.0, 0.0)
            for piece, part in enumerate(pieces):
                spread = jnp.broadcast_to(part[line : line + 1, :], (SUB, width))
                value = jnp.where(sub == ones + 1 + piece, spread, value)
            tail_ref[first + line] = value

    each(height // SUB, block)


def normal_stage(weight_ref, conv_ref, left_ref, right_ref):
    height, groups, _, width = conv_ref.shape
    size = right_ref.shape[0]
    tall = groups * SUB

    def one(row):
        design = conv_ref[row].reshape(tall, width)
        if size > tall:
            design = jnp.concatenate([design, jnp.zeros((size - tall, width), F32)], axis=0)
        weight = jnp.broadcast_to(weight_ref[pl.ds(row, 1), :], (size, width))
        high, low = split_bf16(design * weight, 2)
        where = lanes_of(row, width)
        left_ref[0:size, where] = high
        left_ref[size : 2 * size, where] = low
        right_ref[:, where] = design.astype(BF16)

    each(height, one)
    product = lax.dot_general(
        left_ref[...],
        right_ref[...],
        (((1,), (1,)), ((), ())),
        preferred_element_type=F32,
    )
    return product[0:size] + product[size : 2 * size]


def solve_stage(normal, kernels):
    unknowns = kernels + 1
    width = LANE
    groups = ceil_to(unknowns, SUB) // SUB
    size = normal.shape[1]
    parts = [normal[SUB * g : SUB * (g + 1)] for g in range(groups)]
    if size < width:
        parts = [
            jnp.concatenate([part, jnp.zeros((SUB, width - size), F32)], axis=1)
            for part in parts
        ]

    def pick(value, index, axis):
        where = jnp.full((SUB, width), index, jnp.int32)
        return jnp.take_along_axis(value, where, axis, mode="promise_in_bounds")

    def lane(value, index):
        return pick(value, index, 1)

    def sub(value, index):
        return pick(value, index, 0)

    total = [
        lane(p, unknowns) + (lane(p, unknowns + 1) + lane(p, unknowns + 2)) for p in parts
    ]
    column = lax.broadcasted_iota(jnp.int32, (SUB, width), 1)
    row = lax.broadcasted_iota(jnp.int32, (SUB, width), 0)
    parts = [jnp.where(column == unknowns, t, p) for p, t in zip(parts, total)]
    step = 0
    while step < unknowns:
        if step + 1 < unknowns:
            first, second = step, step + 1
            g0, s0, g1, s1 = first // SUB, first % SUB, second // SUB, second % SUB
            c0 = [lane(p, first) for p in parts]
            c1 = [lane(p, second) for p in parts]
            r0, r1 = sub(parts[g0], s0), sub(parts[g1], s1)
            a, b = lane(r0, first), lane(r0, second)
            e, d = lane(r1, first), lane(r1, second)
            inverse = 1.0 / (a * d - b * e)
            q0 = (d * inverse) * r0 - (b * inverse) * r1
            q1 = (a * inverse) * r1 - (e * inverse) * r0
            parts = [p - x * q0 - y * q1 for p, x, y in zip(parts, c0, c1)]
            parts[g0] = jnp.where(row == s0, q0, parts[g0])
            parts[g1] = jnp.where(row == s1, q1, parts[g1])
            step += 2
        else:
            g0, s0 = step // SUB, step % SUB
            c0 = [lane(p, step) for p in parts]
            r0 = sub(parts[g0], s0)
            q0 = r0 * (1.0 / lane(r0, step))
            parts = [p - x * q0 for p, x in zip(parts, c0)]
            parts[g0] = jnp.where(row == s0, q0, parts[g0])
            step += 1
    values = [lane(p, unknowns) for p in parts]
    last = [jnp.where(row + SUB * g < unknowns, v, 0.0) for g, v in enumerate(values)]
    return last


def residual_stage(values, conv_ref, sci_ref, inverse_ref, diff_ref, out_ref, rows_each):
    height, groups, _, width = conv_ref.shape

    def block(index):
        first = index * SUB
        if not isinstance(first, int):
            first = pl.multiple_of(first, SUB)
        lines = []
        for row in range(SUB):
            total = conv_ref[first + row, 0] * values[0]
            for group in range(1, groups):
                total = total + conv_ref[first + row, group] * values[group]
            lines.append(jnp.sum(total, axis=0, keepdims=True))
        model = jnp.concatenate(lines, axis=0)
        here = pl.ds(first, SUB)
        residual = sci_ref[here, :] - model
        inverse = inverse_ref[here, :]
        diff_ref[0, here, :] = residual * jnp.sqrt(inverse)
        weighted = residual * inverse
        for start in range(0, SUB, rows_each):
            target = (first + start) // rows_each
            out_ref[target, 0:rows_each, :] = weighted[start : start + rows_each]
            out_ref[target, rows_each : 2 * rows_each, :] = inverse[start : start + rows_each]

    each(height // SUB, block)


def store_coefficients(values, coef_ref, unknowns):
    row = lax.broadcasted_iota(jnp.int32, (SUB, LANE), 0)
    column = lax.broadcasted_iota(jnp.int32, (SUB, LANE), 1)
    total = jnp.zeros((SUB, LANE), F32)
    for group, value in enumerate(values):
        total = total + jnp.where(column == row + SUB * group, value, 0.0)
    coef_ref[...] = jnp.sum(total, axis=0, keepdims=True)[:, 0:unknowns]


def fit(tile, edge, science, variance, col_taps, row_taps, stamp_rows, stamp_cols, rows_each, sky):
    height, width = science.shape[1:]
    kernels, tap_count = col_taps.shape
    unknowns = kernels + 1
    groups = ceil_to(unknowns + 3, SUB) // SUB
    size = ceil_to(unknowns + 3, 2 * SUB)
    tall = ceil_to(kernels, 2 * SUB)
    rows, side = chunk_rows(height)
    local = sky == 1
    vmem = pl.BlockSpec(memory_space=pltpu.VMEM)
    smem = pl.BlockSpec(memory_space=pltpu.SMEM)
    params = pltpu.CompilerParams(vmem_limit_bytes=56 * 1024 * 1024)

    def result(shape, dtype=F32):
        return pltpu.VMEM(shape, dtype) if local else jax.ShapeDtypeStruct(shape, dtype)

    def operand(value):
        return pltpu.with_memory_space_constraint(value, pltpu.VMEM) if local else value

    def before(sci, var, ct, rt, sr, sc, flipped, band, weight, inverse, tail, image, pad):
        taps_stage(ct, rt, pad, flipped, band, height)
        weight_stage(sci, var, sr, sc, weight, inverse, tail, kernels)
        image[...] = sci[0]

    flipped, band, weight, inverse, tail, image = pl.pallas_call(
        before,
        out_shape=[
            result((tall, ceil_to(tap_count, SUB)), BF16),
            result((groups, SUB * rows, SUB * (rows + 2 * side)), BF16),
            result((height, width)),
            result((height, width)),
            result((height, SUB, width)),
            result((height, width)),
        ],
        in_specs=[vmem] * 4 + [smem] * 2,
        out_specs=[vmem] * 6,
        scratch_shapes=[pltpu.VMEM((tall, LANE), F32)],
        compiler_params=params,
        name="before",
    )(science, variance, col_taps, row_taps, stamp_rows, stamp_cols)

    conv_shape = (height, groups, SUB, width)
    out_shapes = [
        result((1, height, width)),
        result((1, unknowns)),
        result((height // rows_each, 2 * rows_each, width)),
    ]
    scratch = [
        pltpu.VMEM((groups, SUB * (height + 2 * side), width), BF16),
        pltpu.VMEM((2 * size, height * width), BF16),
        pltpu.VMEM((size, height * width), BF16),
    ]

    def front(tmpl, edges, flipped, band, weight, tail, conv, tmp):
        cols, left, right = tmp
        column_stage(tmpl, edges, flipped, cols, height, tap_count)
        row_stage(band, cols, tail, conv)
        return normal_stage(weight, conv, left, right)

    def back(normal, conv, sci, inverse, diff, coef, out):
        values = solve_stage(normal, kernels)
        store_coefficients(values, coef, unknowns)
        residual_stage(values, conv, sci, inverse, diff, out, rows_each)

    if local:

        def kernel(tmpl, flipped, band, weight, inverse, tail, image, diff, coef, out, conv, *tmp):
            normal = front(tmpl, None, flipped, band, weight, tail, conv, tmp)
            back(normal, conv, image, inverse, diff, coef, out)

        args = (tile, flipped, band, weight, inverse, tail, image)
        return pl.pallas_call(
            kernel,
            out_shape=out_shapes,
            in_specs=[vmem] * 7,
            out_specs=[vmem] * 3,
            scratch_shapes=[pltpu.VMEM(conv_shape, F32)] + scratch,
            compiler_params=params,
            name="fit",
        )(*[operand(arg) for arg in args])

    def first(tmpl, edges, flipped, band, weight, tail, conv, normal, *tmp):
        normal[...] = front(tmpl, edges, flipped, band, weight, tail, conv, tmp)

    conv, normal = pl.pallas_call(
        first,
        out_shape=[result(conv_shape), result((size, size))],
        in_specs=[vmem] * 6,
        out_specs=[vmem] * 2,
        scratch_shapes=scratch,
        compiler_params=params,
        name="fit_normal",
    )(tile.astype(F32), edge.astype(F32), flipped, band, weight, tail)
    normal = lax.psum(normal, "sky")

    def second(normal, conv, sci, inverse, diff, coef, out):
        back(normal[...], conv, sci, inverse, diff, coef, out)

    return pl.pallas_call(
        second,
        out_shape=out_shapes,
        in_specs=[vmem] * 4,
        out_specs=[vmem] * 3,
        compiler_params=params,
        name="fit_solve",
    )(normal, conv, image, inverse)


def sky_edges(tile, margin, sky):
    ends = sky - 1
    width = tile.shape[1]
    head = tile[:, 0:margin]
    tail = tile[:, width - margin :]
    after = lax.ppermute(head, "sky", [(i + 1, i) for i in range(ends)])
    before = lax.ppermute(tail, "sky", [(i, i + 1) for i in range(ends)])
    middle = jnp.zeros((tile.shape[0], width - 2 * margin), tile.dtype)
    return jnp.concatenate([after, middle, before], axis=1)


def solution(mesh):
    visits = mesh.shape["visit"]
    sky = mesh.shape["sky"]

    def on_device(template, science, variance, col_taps, row_taps, stamp_rows, stamp_cols):
        rows_each, width = template.shape
        margin = (col_taps.shape[1] - 1) // 2
        copies = jnp.broadcast_to(template[None], (visits, rows_each, width))
        tile = lax.all_to_all(copies, "visit", 0, 0, tiled=True).reshape(-1, width)
        edge = sky_edges(tile, margin, sky) if sky > 1 else None
        difference, coefficients, shares = fit(
            tile, edge, science, variance, col_taps, row_taps, stamp_rows, stamp_cols, rows_each, sky
        )
        shares = lax.all_to_all(shares, "visit", 0, 0, tiled=True)
        total = jnp.sum(shares, axis=0)
        detection = total[0:rows_each] / jnp.sqrt(total[rows_each:])
        return difference, coefficients, detection

    in_specs = (
        P(("group", "visit"), "sky"),
        P(("group", "visit"), None, "sky"),
        P(("group", "visit"), None, "sky"),
        P(),
        P(),
        P(("group", "visit"), "sky", None),
        P(("group", "visit"), "sky", None),
    )
    out_specs = (
        P(("group", "visit"), None, "sky"),
        P(("group", "visit"), None),
        P(("group", "visit"), "sky"),
    )
    return jax.shard_map(
        on_device, mesh=mesh, in_specs=in_specs, out_specs=out_specs, check_vma=False
    )
```

time: 36.1 us -> 31.8 us (0.88)
  blocking collectives: 10.1 us -> 0 us
  waiting for transfers between devices: 5.07 us -> 9.14 us
  starting transfers between devices: 7.52 us -> 11 us
  Pallas kernels: 8.59 us -> 6.2 us
  local copies, waits for them, and re-layouts: 3.28 us -> 3.8 us
    all_to_all x1 -> x0, blocking collectives: 10.1 us -> none  [on_device(): shares = lax.all_to_all(shares, 'visit', 0, 0, tiled=True)]
    all_to_all x0 -> x1, waiting for transfers between devices: none -> 5.48 us  [on_device(): shares = lax.all_to_all(shares, 'visit', 0, 0, tiled=True)]
    all_to_all x0 -> x1, starting transfers between devices: none -> 3.5 us  [on_device(): shares = lax.all_to_all(shares, 'visit', 0, 0, tiled=True)]
    pallas_call x1 -> x2, Pallas kernels: 8.59 us -> 6.2 us  [the longest x1 4.87 us: fit(): pl.pallas_call(kernel, out_shape=out_shapes, in_specs=[vmem] * 7, out_spe...]
    all_to_all x1, waiting for transfers between devices: 5.07 us -> 3.66 us  [on_device(): tile = lax.all_to_all(copies, 'visit', 0, 0, tiled=True).reshape(-1, width)]
    unnamed x8, local copies, waits for them, and re-layouts: 2.02 us -> 2.54 us
  transfers between devices with their start and end apart: 1 -> 2, of which waited for: 1 -> 2; matrix products, arithmetic and copies ran while one was open for 4% -> 8% of each run, Pallas kernels for 0% -> 4%
where the time goes in v2:
time: 31.8 us; the launch traced here: 31.4 us
  starting transfers between devices  11 us (35%)
  waiting for transfers between devices  9.14 us (29%)
  Pallas kernels  6.2 us (19%)
  local copies, waits for them, and re-layouts  3.8 us (12%)
  between operations  0.67 us (2%)
  other arithmetic  0.6 us (2%)
    all_to_all x1, starting transfers between devices, on_device(): tile = lax.all_to_all(copies, 'visit', 0, 0, tiled=True).reshape(-1, width)  7.52 us
    all_to_all x1, waiting for transfers between devices, on_device(): shares = lax.all_to_all(shares, 'visit', 0, 0, tiled=True)  5.48 us
    pallas_call x1, Pallas kernels, fit(): pl.pallas_call(kernel, out_shape=out_shapes, in_specs=[vmem] * 7, out_spe...  4.87 us
    all_to_all x1, waiting for transfers between devices, on_device(): tile = lax.all_to_all(copies, 'visit', 0, 0, tiled=True).reshape(-1, width)  3.66 us
    all_to_all x1, starting transfers between devices, on_device(): shares = lax.all_to_all(shares, 'visit', 0, 0, tiled=True)  3.5 us
    unnamed x8, local copies, waits for them, and re-layouts  2.54 us
    pallas_call x1, Pallas kernels, fit(): pl.pallas_call(before, out_shape=[result((tall, ceil_to(tap_count, SUB)),...  1.33 us
    broadcast_in_dim x1, local copies, waits for them, and re-layouts, on_device(): copies = jnp.broadcast_to(template[None], (visits, rows_each, width))  1.26 us
  transfers between devices with their start and end apart: 2, of which 2 were waited for; matrix products, arithmetic and copies ran while one was open for 8% of the time, Pallas kernels for 4%

profile of v2, /device:TPU:0, one launch (start us, length us, event | category | flops | bytes accessed | tf_op | source)
XLA Modules:
  0.0 31.4 jit_solution(5108946694980424283)
XLA Ops:
  0.6 1.3 %broadcast_in_dim.2 = bf16[16,2,128]{2,1,0:T(2,128)(2,1)} broadcast(bf16[2,128]{1,0:T(2,128)(2,1)} %param.7), dimensions={1,2} | broadcast | bytes 8704 | tf_op jit(solution)/shard_map/broadcast_in_dim | solution.py:439
  1.9 0.0 copy-start
  1.9 7.5 %all-to-all-start = ((bf16[16,2,128]{2,1,0:T(2,128)(2,1)}), bf16[16,2,128]{2,1,0:T(2,128)(2,1)S(1)}, u32[]{:S(2)}, u32[]{:S(2)}) async-start(bf16[16,2,128]{2,1,0:T(2,128)(2,1)} %broadcast_in_dim.2), calls=%async_computation | async-start | bytes 16384 | tf_op jit(solution)/shard_map/all_to_all | solution.py:440
  9.4 0.0 copy-done
  9.4 0.0 copy-start.1
  9.4 0.7 %copy.10.ct = bf16[49,31]{1,0:T(8,128)(2,1)} copy(bf16[49,31]{0,1:T(8,128)(2,1)S(1)} %copy-done) | data formatting | bytes 6076 | tf_op args[3]
  10.1 0.0 copy-done.1
  10.2 0.7 %copy.11.rt = bf16[49,31]{1,0:T(8,128)(2,1)} copy(bf16[49,31]{0,1:T(8,128)(2,1)S(1)} %copy-done.1) | data formatting | bytes 6076 | tf_op args[4]
  10.9 1.3 %before.1 = (bf16[64,32]{1,0:T(8,128)(2,1)S(1)}, bf16[7,256,256]{2,1,0:T(8,128)(2,1)S(1)}, f32[32,128]{1,0:T(8,128)S(1)}, f32[32,128]{1,0:T(8,128)S(1)}, f32[32,...) custom-call(f32[1,32,128]{2,1,0:T(8,128)} %sci.1, f32[1,32,128]{2,1,0:T(8,128)} %var.1, bf16[49,31]{1,0:T(8,128)(2,1)} %copy.10.ct, ...), custom_call_target="tpu_custom_call" | custom-call | tf_op jit(solution)/shard_map/before/pallas_call | solution.py:337
  12.2 3.7 %all-to-all-done = bf16[16,2,128]{2,1,0:T(2,128)(2,1)S(1)} async-done(((bf16[16,2,128]{2,1,0:T(2,128)(2,1)}), bf16[16,2,128]{2,1,0:T(2,128)(2,1)S(1)}, u32[]{:S(2)}, u32[]{:S(2)}) %all-to-all-start) | async-done | bytes 8224 | tf_op jit(solution)/shard_map/all_to_all | solution.py:440
  15.9 4.9 %fit.1 = (f32[1,32,128]{2,1,0:T(8,128)S(1)}, f32[1,50]{1,0:T(1,128)S(1)}, f32[16,4,128]{2,1,0:T(4,128)}) custom-call(bf16[32,128]{1,0:T(8,128)(2,1)S(1)} %bitcast.1, bf16[64,32]{1,0:T(8,128)(2,1)S(1)} %get-tuple-element.12.flipped, bf16[7,256,256]{2,1,0:T(8,128)(2,1)S(1)} %get-tuple-element.13.band, f32[32,128]{1,0:T(8,128)S(1)} %get-tuple-element.14.weight, ...), custom_call_target="tpu_custom_call" | custom-call | tf_op jit(solution)/shard_map/fit/pallas_call | solution.py:384
  20.7 3.5 %all-to-all-start.1 = ((f32[16,4,128]{2,1,0:T(4,128)}), f32[16,4,128]{2,1,0:T(4,128)S(1)}, u32[]{:S(2)}, u32[]{:S(2)}) async-start(f32[16,4,128]{2,1,0:T(4,128)} %get-tuple-element.20), calls=%async_computation.1 | async-start | bytes 65536 | tf_op jit(solution)/shard_map/all_to_all | solution.py:445
  24.2 0.6 %copy.12 = f32[1,32,128]{2,1,0:T(8,128)} copy(f32[1,32,128]{2,1,0:T(8,128)S(1)} %get-tuple-element.21) | data formatting | bytes 32768
  24.8 0.5 %copy.13 = f32[1,50]{1,0:T(1,128)} copy(f32[1,50]{1,0:T(1,128)S(1)} %get-tuple-element.22) | data formatting | bytes 400
  25.3 5.5 %all-to-all-done.1 = f32[16,4,128]{2,1,0:T(4,128)S(1)} async-done(((f32[16,4,128]{2,1,0:T(4,128)}), f32[16,4,128]{2,1,0:T(4,128)S(1)}, u32[]{:S(2)}, u32[]{:S(2)}) %all-to-all-start.1) | async-done | bytes 32800 | tf_op jit(solution)/shard_map/all_to_all | solution.py:445
  30.8 0.6 %rsqrt_multiply_fusion = f32[2,128]{1,0:T(2,128)} fusion(f32[4,128]{1,0:T(4,128)S(1)} %reduce_sum.9), kind=kLoop, calls=%fused_computation | loop fusion | flops 256 | bytes 3072 | tf_op jit(solution)/shard_map/div | solution.py:447
  (1 shorter events, 0.0 us)
Async XLA Ops:
  1.9 7.5 %copy-start = (bf16[49,31]{0,1:T(8,128)(2,1)S(1)}, bf16[49,31]{0,1:T(8,128)(2,1)}, u32[]{:S(2)}) copy-start(bf16[49,31]{0,1:T(8,128)(2,1)} %param.10) | copy-start | bytes 9118
  1.9 14.0 %all-to-all-start = ((bf16[16,2,128]{2,1,0:T(2,128)(2,1)}), bf16[16,2,128]{2,1,0:T(2,128)(2,1)S(1)}, u32[]{:S(2)}, u32[]{:S(2)}) async-start(bf16[16,2,128]{2,1,0:T(2,128)(2,1)} %broadcast_in_dim.2), calls=%async_computation | async-start | bytes 16384 | tf_op jit(solution)/shard_map/all_to_all | solution.py:440
  9.4 0.7 %copy-start.1 = (bf16[49,31]{0,1:T(8,128)(2,1)S(1)}, bf16[49,31]{0,1:T(8,128)(2,1)}, u32[]{:S(2)}) copy-start(bf16[49,31]{0,1:T(8,128)(2,1)} %param.11) | copy-start | bytes 9118
  20.7 10.1 %all-to-all-start.1 = ((f32[16,4,128]{2,1,0:T(4,128)}), f32[16,4,128]{2,1,0:T(4,128)S(1)}, u32[]{:S(2)}, u32[]{:S(2)}) async-start(f32[16,4,128]{2,1,0:T(4,128)} %get-tuple-element.20), calls=%async_computation.1 | async-start | bytes 65536 | tf_op jit(solution)/shard_map/all_to_all | solution.py:445

commit v3 on v2

--- a/solution.py
+++ b/solution.py
@@ -43,9 +43,10 @@
 
 
 def load_taps(taps_ref, pad_ref):
-    kernels, taps = taps_ref.shape
+    taps, kernels = taps_ref.shape
     pad_ref[...] = jnp.zeros(pad_ref.shape, F32)
-    pad_ref[0:kernels, 0:taps] = taps_ref[...].astype(F32)
+    pad_ref[0:taps, 0:kernels] = taps_ref[...].astype(F32)
+    return pad_ref[...].T
 
 
 def chunk_rows(height):
@@ -54,28 +55,28 @@
 
 
 def taps_stage(col_taps_ref, row_taps_ref, pad_ref, flipped_ref, band_ref, height):
-    tap_count = col_taps_ref.shape[1]
+    tap_count = col_taps_ref.shape[0]
     margin = (tap_count - 1) // 2
     span = ceil_to(tap_count, SUB)
     groups = band_ref.shape[0]
     rows, side = chunk_rows(height)
     wide = SUB * (rows + 2 * side)
-    load_taps(col_taps_ref, pad_ref)
+    taps = load_taps(col_taps_ref, pad_ref)[0 : flipped_ref.shape[0]]
     flip = (
         lax.broadcasted_iota(jnp.int32, (span, span), 0)
         + lax.broadcasted_iota(jnp.int32, (span, span), 1)
         == tap_count - 1
     ).astype(BF16)
     flipped_ref[...] = jnp.dot(
-        pad_ref[:, 0:span].astype(BF16), flip, preferred_element_type=F32
+        taps[:, 0:span].astype(BF16), flip, preferred_element_type=F32
     ).astype(BF16)
-    load_taps(row_taps_ref, pad_ref)
+    taps = load_taps(row_taps_ref, pad_ref)[0 : groups * SUB]
     repeat = (
         lax.broadcasted_iota(jnp.int32, (span, wide), 1) // SUB
         == lax.broadcasted_iota(jnp.int32, (span, wide), 0)
     ).astype(BF16)
     spread = jnp.dot(
-        pad_ref[0 : groups * SUB, 0:span].astype(BF16), repeat, preferred_element_type=F32
+        taps[:, 0:span].astype(BF16), repeat, preferred_element_type=F32
     )
     tall = groups * SUB
     lane = lax.broadcasted_iota(jnp.int32, (tall, wide), 1)
@@ -346,10 +347,10 @@
         ],
         in_specs=[vmem] * 4 + [smem] * 2,
         out_specs=[vmem] * 6,
-        scratch_shapes=[pltpu.VMEM((tall, LANE), F32)],
+        scratch_shapes=[pltpu.VMEM((LANE, LANE), F32)],
         compiler_params=params,
         name="before",
-    )(science, variance, col_taps, row_taps, stamp_rows, stamp_cols)
+    )(science, variance, col_taps.T, row_taps.T, stamp_rows, stamp_cols)
 
     conv_shape = (height, groups, SUB, width)
     out_shapes = [
@@ -429,6 +430,30 @@
     return jnp.concatenate([after, middle, before], axis=1)
 
 
+def gather_results(shares, difference, coefficients):
+    rows_each = shares.shape[1] // 2
+
+    def kernel(shares_ref, diff_ref, coef_ref, diff_out, coef_out, out_ref):
+        diff_out[...] = diff_ref[...]
+        coef_out[...] = coef_ref[...]
+        total = jnp.sum(shares_ref[...], axis=0)
+        out_ref[...] = total[0:rows_each] / jnp.sqrt(total[rows_each:])
+
+    vmem = pl.BlockSpec(memory_space=pltpu.VMEM)
+    args = (shares, difference, coefficients)
+    return pl.pallas_call(
+        kernel,
+        out_shape=[
+            jax.ShapeDtypeStruct(difference.shape, F32),
+            jax.ShapeDtypeStruct(coefficients.shape, F32),
+            jax.ShapeDtypeStruct((rows_each, shares.shape[2]), F32),
+        ],
+        in_specs=[vmem] * 3,
+        out_specs=[vmem] * 3,
+        name="results",
+    )(*[pltpu.with_memory_space_constraint(arg, pltpu.VMEM) for arg in args])
+
+
 def solution(mesh):
     visits = mesh.shape["visit"]
     sky = mesh.shape["sky"]
@@ -443,6 +468,8 @@
             tile, edge, science, variance, col_taps, row_taps, stamp_rows, stamp_cols, rows_each, sky
         )
         shares = lax.all_to_all(shares, "visit", 0, 0, tiled=True)
+        if sky == 1:
+            return gather_results(shares, difference, coefficients)
         total = jnp.sum(shares, axis=0)
         detection = total[0:rows_each] / jnp.sqrt(total[rows_each:])
         return difference, coefficients, detection

time: 31.8 us -> 30 us (0.943)
  blocking collectives: 0 us -> 9.2 us
  waiting for transfers between devices: 9.14 us -> 5.02 us
  starting transfers between devices: 11 us -> 7.39 us
  local copies, waits for them, and re-layouts: 3.8 us -> 1.26 us
  other arithmetic: 0.6 us -> 0 us
    all_to_all x0 -> x1, blocking collectives: none -> 9.2 us  [on_device(): shares = lax.all_to_all(shares, 'visit', 0, 0, tiled=True)]
    all_to_all x1 -> x0, waiting for transfers between devices: 5.48 us -> none  [on_device(): shares = lax.all_to_all(shares, 'visit', 0, 0, tiled=True)]
    all_to_all x1 -> x0, starting transfers between devices: 3.5 us -> none  [on_device(): shares = lax.all_to_all(shares, 'visit', 0, 0, tiled=True)]
    unnamed x8 -> x0, local copies, waits for them, and re-layouts: 2.54 us -> none
    all_to_all x1, waiting for transfers between devices: 3.66 us -> 5.02 us  [on_device(): tile = lax.all_to_all(copies, 'visit', 0, 0, tiled=True).reshape(-1, width)]
    pallas_call x0 -> x1, Pallas kernels: none -> 0.61 us  [gather_results(): pl.pallas_call(kernel, out_shape=[jax.ShapeDtypeStruct(difference.shape,...]
    pallas_call x1, Pallas kernels: 4.87 us -> 4.26 us  [fit(): pl.pallas_call(kernel, out_shape=out_shapes, in_specs=[vmem] * 7, out_spe...]
    div x1 -> x0, other arithmetic: 0.57 us -> none  [on_device(): detection = total[0:rows_each] / jnp.sqrt(total[rows_each:])]
  transfers between devices with their start and end apart: 2 -> 1, of which waited for: 2 -> 1; matrix products, arithmetic and copies ran while one was open for 8% -> 0% of each run, Pallas kernels for 4% -> 4%
where the time goes in v3:
time: 30 us; the launch traced here: 29.7 us
  blocking collectives  9.2 us (31%)
  starting transfers between devices  7.39 us (25%)
  Pallas kernels  6.2 us (21%)
  waiting for transfers between devices  5.02 us (17%)
  local copies, waits for them, and re-layouts  1.26 us (4%)
  between operations  0.65 us (2%)
    all_to_all x1, blocking collectives, on_device(): shares = lax.all_to_all(shares, 'visit', 0, 0, tiled=True)  9.2 us
    all_to_all x1, starting transfers between devices, on_device(): tile = lax.all_to_all(copies, 'visit', 0, 0, tiled=True).reshape(-1, width)  7.39 us
    all_to_all x1, waiting for transfers between devices, on_device(): tile = lax.all_to_all(copies, 'visit', 0, 0, tiled=True).reshape(-1, width)  5.02 us
    pallas_call x1, Pallas kernels, fit(): pl.pallas_call(kernel, out_shape=out_shapes, in_specs=[vmem] * 7, out_spe...  4.26 us
    pallas_call x1, Pallas kernels, fit(): pl.pallas_call(before, out_shape=[result((tall, ceil_to(tap_count, SUB)),...  1.33 us
    broadcast_in_dim x1, local copies, waits for them, and re-layouts, on_device(): copies = jnp.broadcast_to(template[None], (visits, rows_each, width))  1.26 us
    pallas_call x1, Pallas kernels, gather_results(): pl.pallas_call(kernel, out_shape=[jax.ShapeDtypeStruct(difference.shape,...  0.61 us
  transfers between devices with their start and end apart: 1, of which 1 were waited for; matrix products, arithmetic and copies ran while one was open for 0% of the time, Pallas kernels for 4%

profile of v3, /device:TPU:0, one launch (start us, length us, event | category | flops | bytes accessed | tf_op | source)
XLA Modules:
  0.0 29.7 jit_solution(6512370369070438599)
XLA Ops:
  0.6 1.3 %broadcast_in_dim.2 = bf16[16,2,128]{2,1,0:T(2,128)(2,1)} broadcast(bf16[2,128]{1,0:T(2,128)(2,1)} %param.7), dimensions={1,2} | broadcast | bytes 8704 | tf_op jit(solution)/shard_map/broadcast_in_dim | solution.py:464
  1.9 7.4 %all-to-all-start = ((bf16[16,2,128]{2,1,0:T(2,128)(2,1)}), bf16[16,2,128]{2,1,0:T(2,128)(2,1)S(1)}, u32[]{:S(2)}, u32[]{:S(2)}) async-start(bf16[16,2,128]{2,1,0:T(2,128)(2,1)} %broadcast_in_dim.2), calls=%async_computation | async-start | bytes 16384 | tf_op jit(solution)/shard_map/all_to_all | solution.py:465
  9.3 1.3 %before.1 = (bf16[64,32]{1,0:T(8,128)(2,1)S(1)}, bf16[7,256,256]{2,1,0:T(8,128)(2,1)S(1)}, f32[32,128]{1,0:T(8,128)S(1)}, f32[32,128]{1,0:T(8,128)S(1)}, f32[32,...) custom-call(f32[1,32,128]{2,1,0:T(8,128)} %sci.1, f32[1,32,128]{2,1,0:T(8,128)} %var.1, bf16[31,49]{1,0:T(8,128)(2,1)} %bitcast.4, ...), custom_call_target="tpu_custom_call" | custom-call | tf_op jit(solution)/shard_map/before/pallas_call | solution.py:338
  10.6 5.0 %all-to-all-done = bf16[16,2,128]{2,1,0:T(2,128)(2,1)S(1)} async-done(((bf16[16,2,128]{2,1,0:T(2,128)(2,1)}), bf16[16,2,128]{2,1,0:T(2,128)(2,1)S(1)}, u32[]{:S(2)}, u32[]{:S(2)}) %all-to-all-start) | async-done | bytes 8224 | tf_op jit(solution)/shard_map/all_to_all | solution.py:465
  15.6 4.3 %fit.1 = (f32[1,32,128]{2,1,0:T(8,128)S(1)}, f32[1,50]{1,0:T(1,128)S(1)}, f32[16,4,128]{2,1,0:T(4,128)S(1)}) custom-call(bf16[32,128]{1,0:T(8,128)(2,1)S(1)} %bitcast.3, bf16[64,32]{1,0:T(8,128)(2,1)S(1)} %get-tuple-element.12.flipped, bf16[7,256,256]{2,1,0:T(8,128)(2,1)S(1)} %get-tuple-element.13.band, f32[32,128]{1,0:T(8,128)S(1)} %get-tuple-element.14.weight, ...), custom_call_target="tpu_custom_call" | custom-call | tf_op jit(solution)/shard_map/fit/pallas_call | solution.py:385
  19.9 9.2 %all_to_all.10.shares_ref = f32[16,4,128]{2,1,0:T(4,128)S(1)} all-to-all(f32[16,4,128]{2,1,0:T(4,128)S(1)} %get-tuple-element.18), channel_id=1, replica_groups=mesh['group'=2,'visit'=16,'sky'=1] {'visit'}, dimensions={0} | all-to-all | bytes 65536 | tf_op jit(solution)/shard_map/all_to_all | solution.py:470
  29.1 0.6 %results.1 = (f32[1,32,128]{2,1,0:T(8,128)}, f32[1,50]{1,0:T(1,128)}, f32[2,128]{1,0:T(2,128)}) custom-call(f32[16,4,128]{2,1,0:T(4,128)S(1)} %all_to_all.10.shares_ref, f32[1,32,128]{2,1,0:T(8,128)S(1)} %get-tuple-element.19.diff_ref, f32[1,50]{1,0:T(1,128)S(1)} %get-tuple-element.20.coef_ref), custom_call_target="tpu_custom_call" | custom-call | tf_op jit(solution)/shard_map/results/pallas_call | solution.py:444
Async XLA Ops:
  1.9 13.8 %all-to-all-start = ((bf16[16,2,128]{2,1,0:T(2,128)(2,1)}), bf16[16,2,128]{2,1,0:T(2,128)(2,1)S(1)}, u32[]{:S(2)}, u32[]{:S(2)}) async-start(bf16[16,2,128]{2,1,0:T(2,128)(2,1)} %broadcast_in_dim.2), calls=%async_computation | async-start | bytes 16384 | tf_op jit(solution)/shard_map/all_to_all | solution.py:465

commit v4 on v3

--- a/solution.py
+++ b/solution.py
@@ -233,46 +233,69 @@
         where = jnp.full((SUB, width), index, jnp.int32)
         return jnp.take_along_axis(value, where, axis, mode="promise_in_bounds")
 
-    def lane(value, index):
-        return pick(value, index, 1)
-
-    def sub(value, index):
-        return pick(value, index, 0)
-
-    total = [
-        lane(p, unknowns) + (lane(p, unknowns + 1) + lane(p, unknowns + 2)) for p in parts
+    row = lax.broadcasted_iota(jnp.int32, (SUB, width), 0)
+
+    def reduce_pair(values, at, first, second):
+        own, line = at // SUB, at % SUB
+        a, b = pick(first[own], line, 0), pick(second[own], line, 0)
+        d = pick(second[own], line + 1, 0)
+        inverse = 1.0 / (a * d - b * b)
+        a, b, d = a * inverse, b * inverse, d * inverse
+
+        def update(value):
+            r0, r1 = pick(value[own], line, 0), pick(value[own], line + 1, 0)
+            q0 = d * r0 - b * r1
+            q1 = a * r1 - b * r0
+            value = [v - x * q0 - y * q1 for v, x, y in zip(value, first, second)]
+            value[own] = jnp.where(row == line, q0, jnp.where(row == line + 1, q1, value[own]))
+            return value
+
+        return [update(value) for value in values]
+
+    def reduce_last(values, at, first):
+        own, line = at // SUB, at % SUB
+        inverse = 1.0 / pick(first[own], line, 0)
+
+        def update(value):
+            q0 = pick(value[own], line, 0) * inverse
+            value = [v - x * q0 for v, x in zip(value, first)]
+            value[own] = jnp.where(row == line, q0, value[own])
+            return value
+
+        return [update(value) for value in values]
+
+    edges = [0] + list(range(2 - groups % 2, groups + 1, 2))
+    for low, high in zip(edges[:-1], edges[1:]):
+        members = range(low, high)
+        count = min(SUB * high, unknowns) - SUB * low
+        copied = [
+            [pick(part, SUB * low + index, 1) for part in parts] for index in range(count)
+        ]
+        columns = [[one[g] for g in members] for one in copied]
+        block = [parts[g] for g in members]
+        at = 0
+        while at < count:
+            if at + 1 < count:
+                rest = reduce_pair(columns[at + 2 :] + [block], at, columns[at], columns[at + 1])
+                at += 2
+            else:
+                rest = reduce_last(columns[at + 1 :] + [block], at, columns[at])
+                at += 1
+            columns[at:], block = rest[:-1], rest[-1]
+        lines = [pick(block[index // SUB], index % SUB, 0) for index in range(count)]
+        for group in range(groups):
+            if group in members:
+                parts[group] = block[group - low]
+                continue
+            terms = [copied[index][group] * lines[index] for index in range(count)]
+            while len(terms) > 1:
+                terms = [sum(terms[i : i + 2][1:], terms[i]) for i in range(0, len(terms), 2)]
+            parts[group] = parts[group] - terms[0]
+    values = [
+        pick(p, unknowns, 1) + (pick(p, unknowns + 1, 1) + pick(p, unknowns + 2, 1))
+        for p in parts
     ]
-    column = lax.broadcasted_iota(jnp.int32, (SUB, width), 1)
-    row = lax.broadcasted_iota(jnp.int32, (SUB, width), 0)
-    parts = [jnp.where(column == unknowns, t, p) for p, t in zip(parts, total)]
-    step = 0
-    while step < unknowns:
-        if step + 1 < unknowns:
-            first, second = step, step + 1
-            g0, s0, g1, s1 = first // SUB, first % SUB, second // SUB, second % SUB
-            c0 = [lane(p, first) for p in parts]
-            c1 = [lane(p, second) for p in parts]
-            r0, r1 = sub(parts[g0], s0), sub(parts[g1], s1)
-            a, b = lane(r0, first), lane(r0, second)
-            e, d = lane(r1, first), lane(r1, second)
-            inverse = 1.0 / (a * d - b * e)
-            q0 = (d * inverse) * r0 - (b * inverse) * r1
-            q1 = (a * inverse) * r1 - (e * inverse) * r0
-            parts = [p - x * q0 - y * q1 for p, x, y in zip(parts, c0, c1)]
-            parts[g0] = jnp.where(row == s0, q0, parts[g0])
-            parts[g1] = jnp.where(row == s1, q1, parts[g1])
-            step += 2
-        else:
-            g0, s0 = step // SUB, step % SUB
-            c0 = [lane(p, step) for p in parts]
-            r0 = sub(parts[g0], s0)
-            q0 = r0 * (1.0 / lane(r0, step))
-            parts = [p - x * q0 for p, x in zip(parts, c0)]
-            parts[g0] = jnp.where(row == s0, q0, parts[g0])
-            step += 1
-    values = [lane(p, unknowns) for p in parts]
-    last = [jnp.where(row + SUB * g < unknowns, v, 0.0) for g, v in enumerate(values)]
-    return last
+    return [jnp.where(row + SUB * g < unknowns, v, 0.0) for g, v in enumerate(values)]
 
 
 def residual_stage(values, conv_ref, sci_ref, inverse_ref, diff_ref, out_ref, rows_each):

time: 30 us -> 28.5 us (0.950)
  Pallas kernels: 6.2 us -> 4.64 us
    pallas_call x1, Pallas kernels: 4.26 us -> 2.69 us  [fit(): pl.pallas_call(kernel, out_shape=out_shapes, in_specs=[vmem] * 7, out_spe...]
  transfers between devices with their start and end apart: 1 -> 1, of which waited for: 1 -> 1; matrix products, arithmetic and copies ran while one was open for 0% -> 0% of each run, Pallas kernels for 4% -> 5%
where the time goes in v4:
time: 28.5 us; the launch traced here: 28.2 us
  blocking collectives  9.2 us (32%)
  starting transfers between devices  7.39 us (26%)
  waiting for transfers between devices  5.02 us (18%)
  Pallas kernels  4.64 us (16%)
  local copies, waits for them, and re-layouts  1.26 us (4%)
  between operations  0.65 us (2%)
    all_to_all x1, blocking collectives, on_device(): shares = lax.all_to_all(shares, 'visit', 0, 0, tiled=True)  9.2 us
    all_to_all x1, starting transfers between devices, on_device(): tile = lax.all_to_all(copies, 'visit', 0, 0, tiled=True).reshape(-1, width)  7.39 us
    all_to_all x1, waiting for transfers between devices, on_device(): tile = lax.all_to_all(copies, 'visit', 0, 0, tiled=True).reshape(-1, width)  5.02 us
    pallas_call x1, Pallas kernels, fit(): pl.pallas_call(kernel, out_shape=out_shapes, in_specs=[vmem] * 7, out_spe...  2.69 us
    pallas_call x1, Pallas kernels, fit(): pl.pallas_call(before, out_shape=[result((tall, ceil_to(tap_count, SUB)),...  1.33 us
    broadcast_in_dim x1, local copies, waits for them, and re-layouts, on_device(): copies = jnp.broadcast_to(template[None], (visits, rows_each, width))  1.26 us
    pallas_call x1, Pallas kernels, gather_results(): pl.pallas_call(kernel, out_shape=[jax.ShapeDtypeStruct(difference.shape,...  0.61 us
  transfers between devices with their start and end apart: 1, of which 1 were waited for; matrix products, arithmetic and copies ran while one was open for 0% of the time, Pallas kernels for 5%

profile of v4, /device:TPU:0, one launch (start us, length us, event | category | flops | bytes accessed | tf_op | source)
XLA Modules:
  0.0 28.2 jit_solution(14522008496383780643)
XLA Ops:
  0.6 1.3 %broadcast_in_dim.2 = bf16[16,2,128]{2,1,0:T(2,128)(2,1)} broadcast(bf16[2,128]{1,0:T(2,128)(2,1)} %param.7), dimensions={1,2} | broadcast | bytes 8704 | tf_op jit(solution)/shard_map/broadcast_in_dim | solution.py:487
  1.9 7.4 %all-to-all-start = ((bf16[16,2,128]{2,1,0:T(2,128)(2,1)}), bf16[16,2,128]{2,1,0:T(2,128)(2,1)S(1)}, u32[]{:S(2)}, u32[]{:S(2)}) async-start(bf16[16,2,128]{2,1,0:T(2,128)(2,1)} %broadcast_in_dim.2), calls=%async_computation | async-start | bytes 16384 | tf_op jit(solution)/shard_map/all_to_all | solution.py:488
  9.3 1.3 %before.1 = (bf16[64,32]{1,0:T(8,128)(2,1)S(1)}, bf16[7,256,256]{2,1,0:T(8,128)(2,1)S(1)}, f32[32,128]{1,0:T(8,128)S(1)}, f32[32,128]{1,0:T(8,128)S(1)}, f32[32,...) custom-call(f32[1,32,128]{2,1,0:T(8,128)} %sci.1, f32[1,32,128]{2,1,0:T(8,128)} %var.1, bf16[31,49]{1,0:T(8,128)(2,1)} %bitcast.4, ...), custom_call_target="tpu_custom_call" | custom-call | tf_op jit(solution)/shard_map/before/pallas_call | solution.py:361
  10.6 5.0 %all-to-all-done = bf16[16,2,128]{2,1,0:T(2,128)(2,1)S(1)} async-done(((bf16[16,2,128]{2,1,0:T(2,128)(2,1)}), bf16[16,2,128]{2,1,0:T(2,128)(2,1)S(1)}, u32[]{:S(2)}, u32[]{:S(2)}) %all-to-all-start) | async-done | bytes 8224 | tf_op jit(solution)/shard_map/all_to_all | solution.py:488
  15.6 2.7 %fit.1 = (f32[1,32,128]{2,1,0:T(8,128)S(1)}, f32[1,50]{1,0:T(1,128)S(1)}, f32[16,4,128]{2,1,0:T(4,128)S(1)}) custom-call(bf16[32,128]{1,0:T(8,128)(2,1)S(1)} %bitcast.3, bf16[64,32]{1,0:T(8,128)(2,1)S(1)} %get-tuple-element.12.flipped, bf16[7,256,256]{2,1,0:T(8,128)(2,1)S(1)} %get-tuple-element.13.band, f32[32,128]{1,0:T(8,128)S(1)} %get-tuple-element.14.weight, ...), custom_call_target="tpu_custom_call" | custom-call | tf_op jit(solution)/shard_map/fit/pallas_call | solution.py:408
  18.3 9.2 %all_to_all.10.shares_ref = f32[16,4,128]{2,1,0:T(4,128)S(1)} all-to-all(f32[16,4,128]{2,1,0:T(4,128)S(1)} %get-tuple-element.18), channel_id=1, replica_groups=mesh['group'=2,'visit'=16,'sky'=1] {'visit'}, dimensions={0} | all-to-all | bytes 65536 | tf_op jit(solution)/shard_map/all_to_all | solution.py:493
  27.5 0.6 %results.1 = (f32[1,32,128]{2,1,0:T(8,128)}, f32[1,50]{1,0:T(1,128)}, f32[2,128]{1,0:T(2,128)}) custom-call(f32[16,4,128]{2,1,0:T(4,128)S(1)} %all_to_all.10.shares_ref, f32[1,32,128]{2,1,0:T(8,128)S(1)} %get-tuple-element.19.diff_ref, f32[1,50]{1,0:T(1,128)S(1)} %get-tuple-element.20.coef_ref), custom_call_target="tpu_custom_call" | custom-call | tf_op jit(solution)/shard_map/results/pallas_call | solution.py:467
Async XLA Ops:
  1.9 13.8 %all-to-all-start = ((bf16[16,2,128]{2,1,0:T(2,128)(2,1)}), bf16[16,2,128]{2,1,0:T(2,128)(2,1)S(1)}, u32[]{:S(2)}, u32[]{:S(2)}) async-start(bf16[16,2,128]{2,1,0:T(2,128)(2,1)} %broadcast_in_dim.2), calls=%async_computation | async-start | bytes 16384 | tf_op jit(solution)/shard_map/all_to_all | solution.py:488

commit v5 on v4

--- a/solution.py
+++ b/solution.py
@@ -163,24 +163,28 @@
     height, width = weight_ref.shape
     stamps = rows_ref.shape[-1]
     sub = lax.broadcasted_iota(jnp.int32, (SUB, width), 0)
-    col = lax.broadcasted_iota(jnp.int32, (SUB, width), 1)
     ones = kernels % SUB
+
+    def held(starts_ref, length):
+        place = lax.broadcasted_iota(jnp.int32, (length, stamps), 0) - starts_ref[0]
+        return jnp.where((place >= 0) & (place < STAMP), 1.0, 0.0).astype(BF16)
+
+    weight_ref[...] = lax.dot_general(
+        held(rows_ref, height),
+        held(cols_ref, width),
+        (((1,), (1,)), ((), ())),
+        preferred_element_type=F32,
+    )
 
     def block(index):
         first = index * SUB
-        row = sub + first
-        count = jnp.zeros((SUB, width), F32)
-        for stamp in range(stamps):
-            down = row - rows_ref[0, 0, stamp]
-            along = col - cols_ref[0, 0, stamp]
-            held = (down >= 0) & (down < STAMP) & (along >= 0) & (along < STAMP)
-            count = count + jnp.where(held, 1.0, 0.0)
         if not isinstance(first, int):
             first = pl.multiple_of(first, SUB)
-        inverse = 1.0 / var_ref[0, pl.ds(first, SUB), :]
-        inverse_ref[pl.ds(first, SUB), :] = inverse
-        weight_ref[pl.ds(first, SUB), :] = inverse * count
-        pieces = [p.astype(F32) for p in split_bf16(sci_ref[0, pl.ds(first, SUB), :], 3)]
+        here = pl.ds(first, SUB)
+        inverse = 1.0 / var_ref[0, here, :]
+        inverse_ref[here, :] = inverse
+        weight_ref[here, :] = inverse * weight_ref[here, :]
+        pieces = [p.astype(F32) for p in split_bf16(sci_ref[0, here, :], 3)]
         for line in range(SUB):
             value = jnp.where(sub == ones, 1.0, 0.0)
             for piece, part in enumerate(pieces):
@@ -191,29 +195,38 @@
     each(height // SUB, block)
 
 
-def normal_stage(weight_ref, conv_ref, left_ref, right_ref):
+def normal_stage(weight_ref, conv_ref, size):
     height, groups, _, width = conv_ref.shape
-    size = right_ref.shape[0]
     tall = groups * SUB
-
-    def one(row):
-        design = conv_ref[row].reshape(tall, width)
-        if size > tall:
-            design = jnp.concatenate([design, jnp.zeros((size - tall, width), F32)], axis=0)
-        weight = jnp.broadcast_to(weight_ref[pl.ds(row, 1), :], (size, width))
-        high, low = split_bf16(design * weight, 2)
-        where = lanes_of(row, width)
-        left_ref[0:size, where] = high
-        left_ref[size : 2 * size, where] = low
-        right_ref[:, where] = design.astype(BF16)
-
-    each(height, one)
-    product = lax.dot_general(
-        left_ref[...],
-        right_ref[...],
-        (((1,), (1,)), ((), ())),
-        preferred_element_type=F32,
-    )
+    rows = 2
+
+    def chunk(first):
+        left, right = [], []
+        for row in range(rows):
+            design = conv_ref[first + row].reshape(tall, width)
+            if size > tall:
+                design = jnp.concatenate([design, jnp.zeros((size - tall, width), F32)], axis=0)
+            weight = jnp.broadcast_to(weight_ref[pl.ds(first + row, 1), :], (size, width))
+            left.append(jnp.concatenate(split_bf16(design * weight, 2), axis=0))
+            right.append(design.astype(BF16))
+        return lax.dot_general(
+            jnp.concatenate(left, axis=1),
+            jnp.concatenate(right, axis=1),
+            (((1,), (1,)), ((), ())),
+            preferred_element_type=F32,
+        )
+
+    if height <= UNROLL:
+        product = chunk(0)
+        for first in range(rows, height, rows):
+            product = product + chunk(first)
+    else:
+        product = lax.fori_loop(
+            0,
+            height // rows,
+            lambda index, total: total + chunk(index * rows),
+            jnp.zeros((2 * size, size), F32),
+        )
     return product[0:size] + product[size : 2 * size]
 
 
@@ -235,54 +248,46 @@
 
     row = lax.broadcasted_iota(jnp.int32, (SUB, width), 0)
 
-    def reduce_pair(values, at, first, second):
-        own, line = at // SUB, at % SUB
-        a, b = pick(first[own], line, 0), pick(second[own], line, 0)
-        d = pick(second[own], line + 1, 0)
-        inverse = 1.0 / (a * d - b * b)
-        a, b, d = a * inverse, b * inverse, d * inverse
-
-        def update(value):
-            r0, r1 = pick(value[own], line, 0), pick(value[own], line + 1, 0)
-            q0 = d * r0 - b * r1
-            q1 = a * r1 - b * r0
-            value = [v - x * q0 - y * q1 for v, x, y in zip(value, first, second)]
-            value[own] = jnp.where(row == line, q0, jnp.where(row == line + 1, q1, value[own]))
-            return value
-
-        return [update(value) for value in values]
-
-    def reduce_last(values, at, first):
-        own, line = at // SUB, at % SUB
-        inverse = 1.0 / pick(first[own], line, 0)
-
-        def update(value):
-            q0 = pick(value[own], line, 0) * inverse
-            value = [v - x * q0 for v, x in zip(value, first)]
-            value[own] = jnp.where(row == line, q0, value[own])
-            return value
-
-        return [update(value) for value in values]
-
-    edges = [0] + list(range(2 - groups % 2, groups + 1, 2))
+    nothing = jnp.zeros((SUB, width), F32)
+    straight, across = [nothing] * groups, [nothing] * groups
+    edges = [2 * e for e in range(groups // 2)] + [groups]
     for low, high in zip(edges[:-1], edges[1:]):
         members = range(low, high)
-        count = min(SUB * high, unknowns) - SUB * low
+        count = ceil_to(min(SUB * high, unknowns) - SUB * low, 2)
         copied = [
             [pick(part, SUB * low + index, 1) for part in parts] for index in range(count)
         ]
         columns = [[one[g] for g in members] for one in copied]
         block = [parts[g] for g in members]
-        at = 0
-        while at < count:
-            if at + 1 < count:
-                rest = reduce_pair(columns[at + 2 :] + [block], at, columns[at], columns[at + 1])
-                at += 2
-            else:
-                rest = reduce_last(columns[at + 1 :] + [block], at, columns[at])
-                at += 1
-            columns[at:], block = rest[:-1], rest[-1]
-        lines = [pick(block[index // SUB], index % SUB, 0) for index in range(count)]
+        pivots = []
+        for at in range(0, count, 2):
+            own, line = at // SUB, at % SUB
+            first, second = columns[at], columns[at + 1]
+            a, b = pick(first[own], line, 0), pick(second[own], line, 0)
+            d = pick(second[own], line + 1, 0)
+            inverse = 1.0 / (a * d - b * b)
+            a, b, d = a * inverse, b * inverse, d * inverse
+            pivots.append((own, line, a, b, d))
+            here = (row == line) | (row == line + 1)
+            near = [x * d - y * b for x, y in zip(first, second)]
+            far = [y * a - x * b for x, y in zip(first, second)]
+            near[own] = jnp.where(here, 0.0, near[own])
+            far[own] = jnp.where(here, 0.0, far[own])
+
+            def update(value):
+                r0, r1 = pick(value[own], line, 0), pick(value[own], line + 1, 0)
+                return [v - x * r0 - y * r1 for v, x, y in zip(value, near, far)]
+
+            columns[at + 2 :] = [update(value) for value in columns[at + 2 :]]
+            block = update(block)
+            group = low + own
+            diagonal = jnp.where(row == line + 1, a, straight[group])
+            straight[group] = jnp.where(row == line, d, diagonal)
+            across[group] = jnp.where(here, b, across[group])
+        lines = []
+        for own, line, a, b, d in pivots:
+            r0, r1 = pick(block[own], line, 0), pick(block[own], line + 1, 0)
+            lines += [d * r0 - b * r1, a * r1 - b * r0]
         for group in range(groups):
             if group in members:
                 parts[group] = block[group - low]
@@ -291,6 +296,11 @@
             while len(terms) > 1:
                 terms = [sum(terms[i : i + 2][1:], terms[i]) for i in range(0, len(terms), 2)]
             parts[group] = parts[group] - terms[0]
+    other = jnp.where(row % 2 == 0, row + 1, row - 1)
+    parts = [
+        x * p - y * jnp.take_along_axis(p, other, 0, mode="promise_in_bounds")
+        for x, y, p in zip(straight, across, parts)
+    ]
     values = [
         pick(p, unknowns, 1) + (pick(p, unknowns + 1, 1) + pick(p, unknowns + 2, 1))
         for p in parts
@@ -313,7 +323,7 @@
             lines.append(jnp.sum(total, axis=0, keepdims=True))
         model = jnp.concatenate(lines, axis=0)
         here = pl.ds(first, SUB)
-        residual = sci_ref[here, :] - model
+        residual = sci_ref[0, here, :] - model
         inverse = inverse_ref[here, :]
         diff_ref[0, here, :] = residual * jnp.sqrt(inverse)
         weighted = residual * inverse
@@ -336,7 +346,7 @@
 
 def fit(tile, edge, science, variance, col_taps, row_taps, stamp_rows, stamp_cols, rows_each, sky):
     height, width = science.shape[1:]
-    kernels, tap_count = col_taps.shape
+    tap_count, kernels = col_taps.shape
     unknowns = kernels + 1
     groups = ceil_to(unknowns + 3, SUB) // SUB
     size = ceil_to(unknowns + 3, 2 * SUB)
@@ -344,54 +354,36 @@
     rows, side = chunk_rows(height)
     local = sky == 1
     vmem = pl.BlockSpec(memory_space=pltpu.VMEM)
-    smem = pl.BlockSpec(memory_space=pltpu.SMEM)
     params = pltpu.CompilerParams(vmem_limit_bytes=56 * 1024 * 1024)
+    taps = (col_taps, row_taps)
 
     def result(shape, dtype=F32):
         return pltpu.VMEM(shape, dtype) if local else jax.ShapeDtypeStruct(shape, dtype)
 
-    def operand(value):
-        return pltpu.with_memory_space_constraint(value, pltpu.VMEM) if local else value
-
-    def before(sci, var, ct, rt, sr, sc, flipped, band, weight, inverse, tail, image, pad):
-        taps_stage(ct, rt, pad, flipped, band, height)
-        weight_stage(sci, var, sr, sc, weight, inverse, tail, kernels)
-        image[...] = sci[0]
-
-    flipped, band, weight, inverse, tail, image = pl.pallas_call(
-        before,
-        out_shape=[
-            result((tall, ceil_to(tap_count, SUB)), BF16),
-            result((groups, SUB * rows, SUB * (rows + 2 * side)), BF16),
-            result((height, width)),
-            result((height, width)),
-            result((height, SUB, width)),
-            result((height, width)),
-        ],
-        in_specs=[vmem] * 4 + [smem] * 2,
-        out_specs=[vmem] * 6,
-        scratch_shapes=[pltpu.VMEM((LANE, LANE), F32)],
-        compiler_params=params,
-        name="before",
-    )(science, variance, col_taps.T, row_taps.T, stamp_rows, stamp_cols)
-
+    prepared = [
+        ((tall, ceil_to(tap_count, SUB)), BF16),
+        ((groups, SUB * rows, SUB * (rows + 2 * side)), BF16),
+        ((height, width), F32),
+        ((height, width), F32),
+        ((height, SUB, width), F32),
+    ]
+    pad_shape = pltpu.VMEM((LANE, LANE), F32)
     conv_shape = (height, groups, SUB, width)
+    cols_shape = pltpu.VMEM((groups, SUB * (height + 2 * side), width), BF16)
     out_shapes = [
         result((1, height, width)),
         result((1, unknowns)),
         result((height // rows_each, 2 * rows_each, width)),
     ]
-    scratch = [
-        pltpu.VMEM((groups, SUB * (height + 2 * side), width), BF16),
-        pltpu.VMEM((2 * size, height * width), BF16),
-        pltpu.VMEM((size, height * width), BF16),
-    ]
-
-    def front(tmpl, edges, flipped, band, weight, tail, conv, tmp):
-        cols, left, right = tmp
+
+    def before(sci, var, ct, rt, sr, sc, flipped, band, weight, inverse, tail, pad):
+        taps_stage(ct, rt, pad, flipped, band, height)
+        weight_stage(sci, var, sr, sc, weight, inverse, tail, kernels)
+
+    def front(tmpl, edges, flipped, band, weight, tail, conv, cols):
         column_stage(tmpl, edges, flipped, cols, height, tap_count)
         row_stage(band, cols, tail, conv)
-        return normal_stage(weight, conv, left, right)
+        return normal_stage(weight, conv, size)
 
     def back(normal, conv, sci, inverse, diff, coef, out):
         values = solve_stage(normal, kernels)
@@ -400,30 +392,43 @@
 
     if local:
 
-        def kernel(tmpl, flipped, band, weight, inverse, tail, image, diff, coef, out, conv, *tmp):
-            normal = front(tmpl, None, flipped, band, weight, tail, conv, tmp)
-            back(normal, conv, image, inverse, diff, coef, out)
-
-        args = (tile, flipped, band, weight, inverse, tail, image)
+        def kernel(tmpl, sci, var, ct, rt, sr, sc, diff, coef, out, conv, cols, pad, *tables):
+            before(sci, var, ct, rt, sr, sc, *tables, pad)
+            flipped, band, weight, inverse, tail = tables
+            normal = front(tmpl, None, flipped, band, weight, tail, conv, cols)
+            back(normal, conv, sci, inverse, diff, coef, out)
+
+        args = (tile, science, variance) + taps + (stamp_rows, stamp_cols)
         return pl.pallas_call(
             kernel,
             out_shape=out_shapes,
             in_specs=[vmem] * 7,
             out_specs=[vmem] * 3,
-            scratch_shapes=[pltpu.VMEM(conv_shape, F32)] + scratch,
+            scratch_shapes=[pltpu.VMEM(conv_shape, F32), cols_shape, pad_shape]
+            + [pltpu.VMEM(shape, dtype) for shape, dtype in prepared],
             compiler_params=params,
             name="fit",
-        )(*[operand(arg) for arg in args])
-
-    def first(tmpl, edges, flipped, band, weight, tail, conv, normal, *tmp):
-        normal[...] = front(tmpl, edges, flipped, band, weight, tail, conv, tmp)
+        )(*[pltpu.with_memory_space_constraint(arg, pltpu.VMEM) for arg in args])
+
+    flipped, band, weight, inverse, tail = pl.pallas_call(
+        before,
+        out_shape=[result(shape, dtype) for shape, dtype in prepared],
+        in_specs=[vmem] * 6,
+        out_specs=[vmem] * 5,
+        scratch_shapes=[pad_shape],
+        compiler_params=params,
+        name="before",
+    )(science, variance, *taps, stamp_rows, stamp_cols)
+
+    def first(tmpl, edges, flipped, band, weight, tail, conv, normal, cols):
+        normal[...] = front(tmpl, edges, flipped, band, weight, tail, conv, cols)
 
     conv, normal = pl.pallas_call(
         first,
         out_shape=[result(conv_shape), result((size, size))],
         in_specs=[vmem] * 6,
         out_specs=[vmem] * 2,
-        scratch_shapes=scratch,
+        scratch_shapes=[cols_shape],
         compiler_params=params,
         name="fit_normal",
     )(tile.astype(F32), edge.astype(F32), flipped, band, weight, tail)
@@ -439,7 +444,7 @@
         out_specs=[vmem] * 3,
         compiler_params=params,
         name="fit_solve",
-    )(normal, conv, image, inverse)
+    )(normal, conv, science, inverse)
 
 
 def sky_edges(tile, margin, sky):
@@ -451,6 +456,24 @@
     before = lax.ppermute(tail, "sky", [(i, i + 1) for i in range(ends)])
     middle = jnp.zeros((tile.shape[0], width - 2 * margin), tile.dtype)
     return jnp.concatenate([after, middle, before], axis=1)
+
+
+def stage_inputs(lines, count, others):
+    def kernel(*refs):
+        taken, given = refs[: len(refs) // 2], refs[len(refs) // 2 :]
+        given[0][...] = jnp.broadcast_to(taken[0][...][None], given[0].shape)
+        for source, target in zip(taken[1:], given[1:]):
+            target[...] = source[...]
+
+    vmem = pl.BlockSpec(memory_space=pltpu.VMEM)
+    return pl.pallas_call(
+        kernel,
+        out_shape=[pltpu.VMEM((count,) + lines.shape, lines.dtype)]
+        + [pltpu.VMEM(other.shape, other.dtype) for other in others],
+        in_specs=[vmem] * (1 + len(others)),
+        out_specs=[vmem] * (1 + len(others)),
+        name="stage_inputs",
+    )(lines, *others)
 
 
 def gather_results(shares, difference, coefficients):
@@ -484,12 +507,14 @@
     def on_device(template, science, variance, col_taps, row_taps, stamp_rows, stamp_cols):
         rows_each, width = template.shape
         margin = (col_taps.shape[1] - 1) // 2
-        copies = jnp.broadcast_to(template[None], (visits, rows_each, width))
+        others = (science, variance, col_taps.T, row_taps.T, stamp_rows, stamp_cols)
+        if sky == 1:
+            copies, *others = stage_inputs(template, visits, others)
+        else:
+            copies = jnp.broadcast_to(template[None], (visits, rows_each, width))
         tile = lax.all_to_all(copies, "visit", 0, 0, tiled=True).reshape(-1, width)
         edge = sky_edges(tile, margin, sky) if sky > 1 else None
-        difference, coefficients, shares = fit(
-            tile, edge, science, variance, col_taps, row_taps, stamp_rows, stamp_cols, rows_each, sky
-        )
+        difference, coefficients, shares = fit(tile, edge, *others, rows_each, sky)
         shares = lax.all_to_all(shares, "visit", 0, 0, tiled=True)
         if sky == 1:
             return gather_results(shares, difference, coefficients)

time: 28.5 us -> 27.8 us (0.975)
  blocking collectives: 9.2 us -> 22.8 us
  starting transfers between devices: 7.39 us -> 0 us
  waiting for transfers between devices: 5.02 us -> 0 us
  local copies, waits for them, and re-layouts: 1.26 us -> 0 us
  Pallas kernels: 4.64 us -> 4.06 us
    all_to_all x0 -> x1, blocking collectives: none -> 13.6 us  [on_device(): tile = lax.all_to_all(copies, 'visit', 0, 0, tiled=True).reshape(-1, width)]
    all_to_all x1 -> x0, starting transfers between devices: 7.39 us -> none  [on_device(): tile = lax.all_to_all(copies, 'visit', 0, 0, tiled=True).reshape(-1, width)]
    all_to_all x1 -> x0, waiting for transfers between devices: 5.02 us -> none  [on_device(): tile = lax.all_to_all(copies, 'visit', 0, 0, tiled=True).reshape(-1, width)]
    broadcast_in_dim x1 -> x0, local copies, waits for them, and re-layouts: 1.26 us -> none  [on_device(): copies = jnp.broadcast_to(template[None], (visits, rows_each, width))]
    pallas_call x1, Pallas kernels: 1.33 us -> 0.8 us  [stage_inputs(): pl.pallas_call(kernel, out_shape=[pltpu.VMEM((count,) + lines.shape, line...]
  transfers between devices with their start and end apart: 1 -> 0, of which waited for: 1 -> 0; matrix products, arithmetic and copies ran while one was open for 0% -> 0% of each run, Pallas kernels for 5% -> 0%
where the time goes in v5:
time: 27.8 us; the launch traced here: 27.5 us
  blocking collectives  22.8 us (82%)
  Pallas kernels  4.06 us (15%)
  between operations  0.64 us (2%)
    all_to_all x1, blocking collectives, on_device(): tile = lax.all_to_all(copies, 'visit', 0, 0, tiled=True).reshape(-1, width)  13.6 us
    all_to_all x1, blocking collectives, on_device(): shares = lax.all_to_all(shares, 'visit', 0, 0, tiled=True)  9.2 us
    pallas_call x1, Pallas kernels, fit(): pl.pallas_call(kernel, out_shape=out_shapes, in_specs=[vmem] * 7, out_spe...  2.64 us
    pallas_call x1, Pallas kernels, stage_inputs(): pl.pallas_call(kernel, out_shape=[pltpu.VMEM((count,) + lines.shape, line...  0.8 us
    pallas_call x1, Pallas kernels, gather_results(): pl.pallas_call(kernel, out_shape=[jax.ShapeDtypeStruct(difference.shape,...  0.61 us

profile of v5, /device:TPU:0, one launch (start us, length us, event | category | flops | bytes accessed | tf_op | source)
XLA Modules:
  0.0 27.5 jit_solution(4745945327478820455)
XLA Ops:
  0.6 0.8 %stage_inputs.1 = (bf16[16,2,128]{2,1,0:T(2,128)(2,1)S(1)}, f32[1,32,128]{2,1,0:T(8,128)S(1)}, f32[1,32,128]{2,1,0:T(8,128)S(1)}, bf16[31,49]{1,0:T(8,128)(2,1)S...) custom-call(bf16[2,128]{1,0:T(2,128)(2,1)} %refs_0_.1, f32[1,32,128]{2,1,0:T(8,128)} %refs_1_.1, ...), custom_call_target="tpu_custom_call" | custom-call | tf_op jit(solution)/shard_map/stage_inputs/pallas_call | solution.py:469
  1.4 13.6 %all_to_all.10 = bf16[16,2,128]{2,1,0:T(2,128)(2,1)S(1)} all-to-all(bf16[16,2,128]{2,1,0:T(2,128)(2,1)S(1)} %get-tuple-element.13), channel_id=1, replica_groups=mesh['group'=2,'visit'=16,'sky'=1] {'visit'}, dimensions={0} | all-to-all | bytes 16384 | tf_op jit(solution)/shard_map/all_to_all | solution.py:515
  15.1 2.6 %fit.1 = (f32[1,32,128]{2,1,0:T(8,128)S(1)}, f32[1,50]{1,0:T(1,128)S(1)}, f32[16,4,128]{2,1,0:T(4,128)S(1)}) custom-call(bf16[32,128]{1,0:T(8,128)(2,1)S(1)} %bitcast.3, f32[1,32,128]{2,1,0:T(8,128)S(1)} %get-tuple-element.14.sci, f32[1,32,128]{2,1,0:T(8,128)S(1)} %get-tuple-element.15.var, bf16[31,49]{1,0:T(8,128)(2,1)S(1)} %get-tuple-element.16.ct, ...), custom_call_target="tpu_custom_call" | custom-call | tf_op jit(solution)/shard_map/fit/pallas_call | solution.py:402
  17.7 9.2 %all_to_all.11.shares_ref = f32[16,4,128]{2,1,0:T(4,128)S(1)} all-to-all(f32[16,4,128]{2,1,0:T(4,128)S(1)} %get-tuple-element.20), channel_id=1, replica_groups=mesh['group'=2,'visit'=16,'sky'=1] {'visit'}, dimensions={0} | all-to-all | bytes 65536 | tf_op jit(solution)/shard_map/all_to_all | solution.py:518
  26.9 0.6 %results.1 = (f32[1,32,128]{2,1,0:T(8,128)}, f32[1,50]{1,0:T(1,128)}, f32[2,128]{1,0:T(2,128)}) custom-call(f32[16,4,128]{2,1,0:T(4,128)S(1)} %all_to_all.11.shares_ref, f32[1,32,128]{2,1,0:T(8,128)S(1)} %get-tuple-element.21.diff_ref, f32[1,50]{1,0:T(1,128)S(1)} %get-tuple-element.22.coef_ref), custom_call_target="tpu_custom_call" | custom-call | tf_op jit(solution)/shard_map/results/pallas_call | solution.py:490

commit v6 on v5

--- a/solution.py
+++ b/solution.py
@@ -54,46 +54,67 @@
     return rows, (0 if rows == height else CHUNK // 2)
 
 
+def halves(shape):
+    return lax.broadcasted_iota(jnp.int32, shape, 0) % SUB < SUB // 2
+
+
+def turned(value):
+    tiles = [value[at : at + SUB] for at in range(0, value.shape[0], SUB)]
+    return jnp.concatenate([pltpu.roll(tile, SUB // 2, 0) for tile in tiles], axis=0)
+
+
 def taps_stage(col_taps_ref, row_taps_ref, pad_ref, flipped_ref, band_ref, height):
     tap_count = col_taps_ref.shape[0]
     margin = (tap_count - 1) // 2
     span = ceil_to(tap_count, SUB)
     groups = band_ref.shape[0]
     rows, side = chunk_rows(height)
-    wide = SUB * (rows + 2 * side)
-    taps = load_taps(col_taps_ref, pad_ref)[0 : flipped_ref.shape[0]]
+    reach = rows + 2 * side
+    wide = SUB // 2 * reach
+    tall = groups * SUB
+    taps = load_taps(col_taps_ref, pad_ref)[0 : flipped_ref.shape[1], 0:span]
     flip = (
         lax.broadcasted_iota(jnp.int32, (span, span), 0)
         + lax.broadcasted_iota(jnp.int32, (span, span), 1)
         == tap_count - 1
     ).astype(BF16)
-    flipped_ref[...] = jnp.dot(
-        taps[:, 0:span].astype(BF16), flip, preferred_element_type=F32
-    ).astype(BF16)
-    taps = load_taps(row_taps_ref, pad_ref)[0 : groups * SUB]
-    repeat = (
-        lax.broadcasted_iota(jnp.int32, (span, wide), 1) // SUB
-        == lax.broadcasted_iota(jnp.int32, (span, wide), 0)
-    ).astype(BF16)
-    spread = jnp.dot(
-        taps[:, 0:span].astype(BF16), repeat, preferred_element_type=F32
-    )
-    tall = groups * SUB
-    lane = lax.broadcasted_iota(jnp.int32, (tall, wide), 1)
-    own = lane % SUB == lax.broadcasted_iota(jnp.int32, (tall, wide), 0) % SUB
-    spread = jnp.where(own, spread, 0.0)
-    place = lane // SUB - side
-
-    def line(row):
-        moved = pltpu.roll(spread, (SUB * (row - margin + side)) % wide, 1)
-        return jnp.where((place >= row - margin) & (place <= row + margin), moved, 0.0)
-
-    for row in range(0, rows, 2):
-        first, second = line(row), line(row + 1)
-        for group in range(groups):
-            here = slice(SUB * group, SUB * (group + 1))
-            both = jnp.concatenate([first[here], second[here]], axis=0)
-            band_ref[group, SUB * row : SUB * (row + 2), :] = both.astype(BF16)
+    reversed_taps = jnp.dot(taps.astype(BF16), flip, preferred_element_type=F32)
+    flipped_ref[0] = reversed_taps.astype(BF16)
+    flipped_ref[1] = turned(reversed_taps).astype(BF16)
+    taps = load_taps(row_taps_ref, pad_ref)[0:tall, 0:span]
+    other = turned(taps)
+    lower = halves((tall, span))
+    tap = lax.broadcasted_iota(jnp.int32, (span, wide), 0)
+    lane = lax.broadcasted_iota(jnp.int32, (span, wide), 1)
+    line = lax.broadcasted_iota(jnp.int32, (tall, wide), 0)
+    along = lax.broadcasted_iota(jnp.int32, (tall, wide), 1)
+    for half in range(2):
+        four = jnp.where(lower, taps, other) if half == 0 else jnp.where(lower, other, taps)
+
+        def second(index):
+            late = index % SUB >= SUB // 2
+            return jnp.where(late, 1 - half, half)
+
+        def base(shift):
+            source = 2 * (lane // SUB) + second(lane) - shift - side + margin
+            repeat = ((source + reach) % reach == tap).astype(BF16)
+            return jnp.dot(four.astype(BF16), repeat, preferred_element_type=F32)
+
+        spread = jnp.where(second(line) == 1, base(1), base(0))
+        spread = jnp.where(line % (SUB // 2) == along % (SUB // 2), spread, 0.0)
+        place = 2 * (along // SUB) + second(along) - second(line) - side
+
+        def pair(index):
+            moved = pltpu.roll(spread, SUB * index, 1) if index else spread
+            offset = place - 2 * index
+            return jnp.where((offset >= -margin) & (offset <= margin), moved, 0.0)
+
+        for index in range(0, rows // 2, 2):
+            first, next_one = pair(index), pair(index + 1)
+            for group in range(groups):
+                here = slice(SUB * group, SUB * (group + 1))
+                both = jnp.concatenate([first[here], next_one[here]], axis=0)
+                band_ref[group, half, SUB * index : SUB * (index + 2), :] = both.astype(BF16)
 
 
 def column_stage(tmpl_ref, edge_ref, flipped_ref, cols_ref, height, tap_count):
@@ -102,15 +123,15 @@
     span = ceil_to(tap_count, SUB)
     groups = cols_ref.shape[0]
     _, side = chunk_rows(height)
-    taps = flipped_ref[...]
     place = lax.broadcasted_iota(jnp.int32, (span, width), 1) + (
         margin - lax.broadcasted_iota(jnp.int32, (span, width), 0)
     )
     inside = (place >= 0) & (place < width)
+    lower = halves((SUB, width))
     if side:
-        nothing = jnp.zeros((groups, SUB * side, width), BF16)
-        cols_ref[:, 0 : SUB * side, :] = nothing
-        cols_ref[:, SUB * (side + height) :, :] = nothing
+        nothing = jnp.zeros((groups, 2, SUB // 2 * side, width), BF16)
+        cols_ref[:, :, 0 : SUB // 2 * side, :] = nothing
+        cols_ref[:, :, SUB // 2 * (side + height) :, :] = nothing
 
     def shifted(row):
         line = jnp.broadcast_to(tmpl_ref[pl.ds(row, 1), :].astype(F32), (span, width))
@@ -121,40 +142,57 @@
         other = pltpu.roll(other, width - margin, 1, stride=1, stride_axis=0)
         return jnp.where(inside, line, other).astype(BF16)
 
-    def pair(index):
-        both = jnp.concatenate([shifted(2 * index), shifted(2 * index + 1)], axis=1)
-        result = jnp.dot(taps, both, preferred_element_type=F32)
-        start = SUB * (2 * index + side)
+    def quad(index):
+        results = []
+        for odd in range(2):
+            row = 4 * index + odd
+            both = jnp.concatenate([shifted(row), shifted(row + 2)], axis=1)
+            results.append(jnp.dot(flipped_ref[odd], both, preferred_element_type=F32))
+        start = 2 * SUB * index + SUB // 2 * side
         if not isinstance(start, int):
             start = pl.multiple_of(start, 2 * SUB)
         for group in range(groups):
-            here = result[SUB * group : SUB * (group + 1)]
-            two = jnp.concatenate([here[:, 0:width], here[:, width:]], axis=0)
-            cols_ref[group, pl.ds(start, 2 * SUB), :] = two.astype(BF16)
-
-    each(height // 2, pair)
+            even, odd = [value[SUB * group : SUB * (group + 1)] for value in results]
+            even, odd = [[v[:, 0:width], v[:, width:]] for v in (even, odd)]
+            for half in range(2):
+                tiles = [
+                    jnp.where(lower, e, o) if half == 0 else jnp.where(lower, o, e)
+                    for e, o in zip(even, odd)
+                ]
+                two = jnp.concatenate(tiles, axis=0)
+                cols_ref[group, half, pl.ds(start, 2 * SUB), :] = two.astype(BF16)
+
+    each(height // 4, quad)
 
 
 def row_stage(band_ref, cols_ref, tail_ref, conv_ref):
     height, groups, _, width = conv_ref.shape
     rows, side = chunk_rows(height)
+    lower = halves((SUB, width))
 
     def chunk(index):
         first = index * rows
-        start = SUB * first
+        start = SUB // 2 * first
         if not isinstance(start, int):
-            start = pl.multiple_of(start, SUB * rows)
+            start = pl.multiple_of(start, SUB // 2 * rows)
         for group in range(groups):
-            result = jnp.dot(
-                band_ref[group],
-                cols_ref[group, pl.ds(start, SUB * (rows + 2 * side)), :],
-                preferred_element_type=F32,
-            )
-            for row in range(rows):
-                value = result[SUB * row : SUB * (row + 1)].astype(BF16).astype(F32)
-                if group == groups - 1:
-                    value = value + tail_ref[first + row]
-                conv_ref[first + row, group] = value
+            near, far = [
+                jnp.dot(
+                    band_ref[group, half],
+                    cols_ref[group, half, pl.ds(start, SUB // 2 * (rows + 2 * side)), :],
+                    preferred_element_type=F32,
+                )
+                for half in range(2)
+            ]
+            for pair in range(rows // 2):
+                here = slice(SUB * pair, SUB * (pair + 1))
+                even = jnp.where(lower, near[here], far[here])
+                odd = pltpu.roll(jnp.where(lower, far[here], near[here]), SUB // 2, 0)
+                for row, value in ((2 * pair, even), (2 * pair + 1, odd)):
+                    value = value.astype(BF16).astype(F32)
+                    if group == groups - 1:
+                        value = value + tail_ref[first + row]
+                    conv_ref[first + row, group] = value
 
     each(height // rows, chunk)
 
@@ -361,15 +399,15 @@
         return pltpu.VMEM(shape, dtype) if local else jax.ShapeDtypeStruct(shape, dtype)
 
     prepared = [
-        ((tall, ceil_to(tap_count, SUB)), BF16),
-        ((groups, SUB * rows, SUB * (rows + 2 * side)), BF16),
+        ((2, tall, ceil_to(tap_count, SUB)), BF16),
+        ((groups, 2, SUB // 2 * rows, SUB // 2 * (rows + 2 * side)), BF16),
         ((height, width), F32),
         ((height, width), F32),
         ((height, SUB, width), F32),
     ]
     pad_shape = pltpu.VMEM((LANE, LANE), F32)
     conv_shape = (height, groups, SUB, width)
-    cols_shape = pltpu.VMEM((groups, SUB * (height + 2 * side), width), BF16)
+    cols_shape = pltpu.VMEM((groups, 2, SUB // 2 * (height + 2 * side), width), BF16)
     out_shapes = [
         result((1, height, width)),
         result((1, unknowns)),

time: 27.8 us -> 27.5 us (0.989)
  no operation moved by 1% of the time
where the time goes in v6:
time: 27.5 us; the launch traced here: 27.3 us
  blocking collectives  22.8 us (83%)
  Pallas kernels  3.8 us (14%)
  between operations  0.64 us (2%)
    all_to_all x1, blocking collectives, on_device(): tile = lax.all_to_all(copies, 'visit', 0, 0, tiled=True).reshape(-1, width)  13.6 us
    all_to_all x1, blocking collectives, on_device(): shares = lax.all_to_all(shares, 'visit', 0, 0, tiled=True)  9.2 us
    pallas_call x1, Pallas kernels, fit(): pl.pallas_call(kernel, out_shape=out_shapes, in_specs=[vmem] * 7, out_spe...  2.38 us
    pallas_call x1, Pallas kernels, stage_inputs(): pl.pallas_call(kernel, out_shape=[pltpu.VMEM((count,) + lines.shape, line...  0.8 us
    pallas_call x1, Pallas kernels, gather_results(): pl.pallas_call(kernel, out_shape=[jax.ShapeDtypeStruct(difference.shape,...  0.61 us

profile of v6, /device:TPU:0, one launch (start us, length us, event | category | flops | bytes accessed | tf_op | source)
XLA Modules:
  0.0 27.3 jit_solution(10849902114477659924)
XLA Ops:
  0.6 0.8 %stage_inputs.1 = (bf16[16,2,128]{2,1,0:T(2,128)(2,1)S(1)}, f32[1,32,128]{2,1,0:T(8,128)S(1)}, f32[1,32,128]{2,1,0:T(8,128)S(1)}, bf16[31,49]{1,0:T(8,128)(2,1)S...) custom-call(bf16[2,128]{1,0:T(2,128)(2,1)} %refs_0_.1, f32[1,32,128]{2,1,0:T(8,128)} %refs_1_.1, ...), custom_call_target="tpu_custom_call" | custom-call | tf_op jit(solution)/shard_map/stage_inputs/pallas_call | solution.py:507
  1.4 13.6 %all_to_all.10 = bf16[16,2,128]{2,1,0:T(2,128)(2,1)S(1)} all-to-all(bf16[16,2,128]{2,1,0:T(2,128)(2,1)S(1)} %get-tuple-element.13), channel_id=1, replica_groups=mesh['group'=2,'visit'=16,'sky'=1] {'visit'}, dimensions={0} | all-to-all | bytes 16384 | tf_op jit(solution)/shard_map/all_to_all | solution.py:553
  15.1 2.4 %fit.1 = (f32[1,32,128]{2,1,0:T(8,128)S(1)}, f32[1,50]{1,0:T(1,128)S(1)}, f32[16,4,128]{2,1,0:T(4,128)S(1)}) custom-call(bf16[32,128]{1,0:T(8,128)(2,1)S(1)} %bitcast.3, f32[1,32,128]{2,1,0:T(8,128)S(1)} %get-tuple-element.14.sci, f32[1,32,128]{2,1,0:T(8,128)S(1)} %get-tuple-element.15.var, bf16[31,49]{1,0:T(8,128)(2,1)S(1)} %get-tuple-element.16.ct, ...), custom_call_target="tpu_custom_call" | custom-call | tf_op jit(solution)/shard_map/fit/pallas_call | solution.py:440
  17.4 9.2 %all_to_all.11.shares_ref = f32[16,4,128]{2,1,0:T(4,128)S(1)} all-to-all(f32[16,4,128]{2,1,0:T(4,128)S(1)} %get-tuple-element.20), channel_id=1, replica_groups=mesh['group'=2,'visit'=16,'sky'=1] {'visit'}, dimensions={0} | all-to-all | bytes 65536 | tf_op jit(solution)/shard_map/all_to_all | solution.py:556
  26.7 0.6 %results.1 = (f32[1,32,128]{2,1,0:T(8,128)}, f32[1,50]{1,0:T(1,128)}, f32[2,128]{1,0:T(2,128)}) custom-call(f32[16,4,128]{2,1,0:T(4,128)S(1)} %all_to_all.11.shares_ref, f32[1,32,128]{2,1,0:T(8,128)S(1)} %get-tuple-element.21.diff_ref, f32[1,50]{1,0:T(1,128)S(1)} %get-tuple-element.22.coef_ref), custom_call_target="tpu_custom_call" | custom-call | tf_op jit(solution)/shard_map/results/pallas_call | solution.py:528

commit v7 on v6

--- a/solution.py
+++ b/solution.py
@@ -55,7 +55,7 @@
 
 
 def halves(shape):
-    return lax.broadcasted_iota(jnp.int32, shape, 0) % SUB < SUB // 2
+    return (lax.broadcasted_iota(jnp.int32, shape, 0) & (SUB - 1)) < SUB // 2
 
 
 def turned(value):
@@ -86,35 +86,43 @@
     lower = halves((tall, span))
     tap = lax.broadcasted_iota(jnp.int32, (span, wide), 0)
     lane = lax.broadcasted_iota(jnp.int32, (span, wide), 1)
-    line = lax.broadcasted_iota(jnp.int32, (tall, wide), 0)
-    along = lax.broadcasted_iota(jnp.int32, (tall, wide), 1)
+    sub = lax.broadcasted_iota(jnp.int32, (SUB, wide), 0)
+    along = lax.broadcasted_iota(jnp.int32, (SUB, wide), 1)
+    own = (sub & (SUB // 2 - 1)) == (along & (SUB // 2 - 1))
+    bit = (SUB // 2).bit_length() - 1
     for half in range(2):
         four = jnp.where(lower, taps, other) if half == 0 else jnp.where(lower, other, taps)
 
-        def second(index):
-            late = index % SUB >= SUB // 2
-            return jnp.where(late, 1 - half, half)
+        def line_of(index):
+            return 2 * (index >> (bit + 1)) + (((index >> bit) & 1) ^ half)
 
         def base(shift):
-            source = 2 * (lane // SUB) + second(lane) - shift - side + margin
-            repeat = ((source + reach) % reach == tap).astype(BF16)
+            source = line_of(lane) - shift - side + margin
+            source = jnp.where(source >= reach, source - reach, source)
+            source = jnp.where(source < 0, source + reach, source)
+            repeat = jnp.where(source == tap, 1.0, 0.0).astype(BF16)
             return jnp.dot(four.astype(BF16), repeat, preferred_element_type=F32)
 
-        spread = jnp.where(second(line) == 1, base(1), base(0))
-        spread = jnp.where(line % (SUB // 2) == along % (SUB // 2), spread, 0.0)
-        place = 2 * (along // SUB) + second(along) - second(line) - side
-
-        def pair(index):
-            moved = pltpu.roll(spread, SUB * index, 1) if index else spread
-            offset = place - 2 * index
-            return jnp.where((offset >= -margin) & (offset <= margin), moved, 0.0)
+        first, second = base(0), base(1)
+        place = line_of(along) - line_of(sub) - side
+        late = line_of(sub) == 1
+        spread = []
+        for group in range(groups):
+            here = slice(SUB * group, SUB * (group + 1))
+            spread.append(jnp.where(own, jnp.where(late, second[here], first[here]), 0.0))
 
         for index in range(0, rows // 2, 2):
-            first, next_one = pair(index), pair(index + 1)
+            inside = [
+                (place >= 2 * pair - margin) & (place <= 2 * pair + margin)
+                for pair in (index, index + 1)
+            ]
             for group in range(groups):
-                here = slice(SUB * group, SUB * (group + 1))
-                both = jnp.concatenate([first[here], next_one[here]], axis=0)
-                band_ref[group, half, SUB * index : SUB * (index + 2), :] = both.astype(BF16)
+                both = [
+                    jnp.where(inside[pair], pltpu.roll(spread[group], SUB * (index + pair), 1), 0.0)
+                    for pair in range(2)
+                ]
+                both = jnp.concatenate(both, axis=0).astype(BF16)
+                band_ref[group, half, SUB * index : SUB * (index + 2), :] = both
 
 
 def column_stage(tmpl_ref, edge_ref, flipped_ref, cols_ref, height, tap_count):
@@ -166,7 +174,8 @@
 
 
 def row_stage(band_ref, cols_ref, tail_ref, conv_ref):
-    height, groups, _, width = conv_ref.shape
+    height, _, width = conv_ref.shape
+    groups = band_ref.shape[0]
     rows, side = chunk_rows(height)
     lower = halves((SUB, width))
 
@@ -175,24 +184,36 @@
         start = SUB // 2 * first
         if not isinstance(start, int):
             start = pl.multiple_of(start, SUB // 2 * rows)
-        for group in range(groups):
-            near, far = [
-                jnp.dot(
-                    band_ref[group, half],
-                    cols_ref[group, half, pl.ds(start, SUB // 2 * (rows + 2 * side)), :],
-                    preferred_element_type=F32,
-                )
-                for half in range(2)
+        for group in range(0, groups, 2):
+            members = range(group, min(group + 2, groups))
+            pairs = [
+                [
+                    jnp.dot(
+                        band_ref[g, half],
+                        cols_ref[g, half, pl.ds(start, SUB // 2 * (rows + 2 * side)), :],
+                        preferred_element_type=F32,
+                    )
+                    for half in range(2)
+                ]
+                for g in members
             ]
             for pair in range(rows // 2):
                 here = slice(SUB * pair, SUB * (pair + 1))
-                even = jnp.where(lower, near[here], far[here])
-                odd = pltpu.roll(jnp.where(lower, far[here], near[here]), SUB // 2, 0)
-                for row, value in ((2 * pair, even), (2 * pair + 1, odd)):
-                    value = value.astype(BF16).astype(F32)
-                    if group == groups - 1:
-                        value = value + tail_ref[first + row]
-                    conv_ref[first + row, group] = value
+                both = []
+                for near, far in pairs:
+                    even = jnp.where(lower, near[here], far[here])
+                    odd = pltpu.roll(jnp.where(lower, far[here], near[here]), SUB // 2, 0)
+                    both.append((even, odd))
+                for half in range(2):
+                    row = first + 2 * pair + half
+                    tiles = [one[half] for one in both]
+                    if members[-1] == groups - 1:
+                        tiles[-1] = tiles[-1] + tail_ref[row]
+                    if len(tiles) == 1:
+                        tiles.append(jnp.zeros((SUB, width), F32))
+                    conv_ref[row, SUB * group : SUB * (group + 2), :] = jnp.concatenate(
+                        tiles, axis=0
+                    ).astype(BF16)
 
     each(height // rows, chunk)
 
@@ -234,19 +255,16 @@
 
 
 def normal_stage(weight_ref, conv_ref, size):
-    height, groups, _, width = conv_ref.shape
-    tall = groups * SUB
+    height, _, width = conv_ref.shape
     rows = 2
 
     def chunk(first):
         left, right = [], []
         for row in range(rows):
-            design = conv_ref[first + row].reshape(tall, width)
-            if size > tall:
-                design = jnp.concatenate([design, jnp.zeros((size - tall, width), F32)], axis=0)
+            design = conv_ref[first + row]
             weight = jnp.broadcast_to(weight_ref[pl.ds(first + row, 1), :], (size, width))
-            left.append(jnp.concatenate(split_bf16(design * weight, 2), axis=0))
-            right.append(design.astype(BF16))
+            left.append(jnp.concatenate(split_bf16(design.astype(F32) * weight, 2), axis=0))
+            right.append(design)
         return lax.dot_general(
             jnp.concatenate(left, axis=1),
             jnp.concatenate(right, axis=1),
@@ -334,7 +352,7 @@
             while len(terms) > 1:
                 terms = [sum(terms[i : i + 2][1:], terms[i]) for i in range(0, len(terms), 2)]
             parts[group] = parts[group] - terms[0]
-    other = jnp.where(row % 2 == 0, row + 1, row - 1)
+    other = row ^ 1
     parts = [
         x * p - y * jnp.take_along_axis(p, other, 0, mode="promise_in_bounds")
         for x, y, p in zip(straight, across, parts)
@@ -347,7 +365,7 @@
 
 
 def residual_stage(values, conv_ref, sci_ref, inverse_ref, diff_ref, out_ref, rows_each):
-    height, groups, _, width = conv_ref.shape
+    height, _, width = conv_ref.shape
 
     def block(index):
         first = index * SUB
@@ -355,9 +373,10 @@
             first = pl.multiple_of(first, SUB)
         lines = []
         for row in range(SUB):
-            total = conv_ref[first + row, 0] * values[0]
-            for group in range(1, groups):
-                total = total + conv_ref[first + row, group] * values[group]
+            design = conv_ref[first + row].astype(F32)
+            total = design[0:SUB] * values[0]
+            for group in range(1, len(values)):
+                total = total + design[SUB * group : SUB * (group + 1)] * values[group]
             lines.append(jnp.sum(total, axis=0, keepdims=True))
         model = jnp.concatenate(lines, axis=0)
         here = pl.ds(first, SUB)
@@ -406,7 +425,7 @@
         ((height, SUB, width), F32),
     ]
     pad_shape = pltpu.VMEM((LANE, LANE), F32)
-    conv_shape = (height, groups, SUB, width)
+    conv_shape = (height, size, width)
     cols_shape = pltpu.VMEM((groups, 2, SUB // 2 * (height + 2 * side), width), BF16)
     out_shapes = [
         result((1, height, width)),
@@ -442,7 +461,7 @@
             out_shape=out_shapes,
             in_specs=[vmem] * 7,
             out_specs=[vmem] * 3,
-            scratch_shapes=[pltpu.VMEM(conv_shape, F32), cols_shape, pad_shape]
+            scratch_shapes=[pltpu.VMEM(conv_shape, BF16), cols_shape, pad_shape]
             + [pltpu.VMEM(shape, dtype) for shape, dtype in prepared],
             compiler_params=params,
             name="fit",
@@ -463,7 +482,7 @@
 
     conv, normal = pl.pallas_call(
         first,
-        out_shape=[result(conv_shape), result((size, size))],
+        out_shape=[result(conv_shape, BF16), result((size, size))],
         in_specs=[vmem] * 6,
         out_specs=[vmem] * 2,
         scratch_shapes=[cols_shape],

time: 27.5 us -> 27.4 us (level)
  no operation moved by 1% of the time
where the time goes in v7:
time: 27.4 us; the launch traced here: 27.1 us
  blocking collectives  22.8 us (83%)
  Pallas kernels  3.66 us (13%)
  between operations  0.64 us (2%)
    all_to_all x1, blocking collectives, on_device(): tile = lax.all_to_all(copies, 'visit', 0, 0, tiled=True).reshape(-1, width)  13.6 us
    all_to_all x1, blocking collectives, on_device(): shares = lax.all_to_all(shares, 'visit', 0, 0, tiled=True)  9.2 us
    pallas_call x1, Pallas kernels, fit(): pl.pallas_call(kernel, out_shape=out_shapes, in_specs=[vmem] * 7, out_spe...  2.24 us
    pallas_call x1, Pallas kernels, stage_inputs(): pl.pallas_call(kernel, out_shape=[pltpu.VMEM((count,) + lines.shape, line...  0.8 us
    pallas_call x1, Pallas kernels, gather_results(): pl.pallas_call(kernel, out_shape=[jax.ShapeDtypeStruct(difference.shape,...  0.61 us

profile of v7, /device:TPU:0, one launch (start us, length us, event | category | flops | bytes accessed | tf_op | source)
XLA Modules:
  0.0 27.1 jit_solution(5675106757835448663)
XLA Ops:
  0.6 0.8 %stage_inputs.1 = (bf16[16,2,128]{2,1,0:T(2,128)(2,1)S(1)}, f32[1,32,128]{2,1,0:T(8,128)S(1)}, f32[1,32,128]{2,1,0:T(8,128)S(1)}, bf16[31,49]{1,0:T(8,128)(2,1)S...) custom-call(bf16[2,128]{1,0:T(2,128)(2,1)} %refs_0_.1, f32[1,32,128]{2,1,0:T(8,128)} %refs_1_.1, ...), custom_call_target="tpu_custom_call" | custom-call | tf_op jit(solution)/shard_map/stage_inputs/pallas_call | solution.py:526
  1.4 13.6 %all_to_all.10 = bf16[16,2,128]{2,1,0:T(2,128)(2,1)S(1)} all-to-all(bf16[16,2,128]{2,1,0:T(2,128)(2,1)S(1)} %get-tuple-element.13), channel_id=1, replica_groups=mesh['group'=2,'visit'=16,'sky'=1] {'visit'}, dimensions={0} | all-to-all | bytes 16384 | tf_op jit(solution)/shard_map/all_to_all | solution.py:572
  15.1 2.2 %fit.1 = (f32[1,32,128]{2,1,0:T(8,128)S(1)}, f32[1,50]{1,0:T(1,128)S(1)}, f32[16,4,128]{2,1,0:T(4,128)S(1)}) custom-call(bf16[32,128]{1,0:T(8,128)(2,1)S(1)} %bitcast.3, f32[1,32,128]{2,1,0:T(8,128)S(1)} %get-tuple-element.14.sci, f32[1,32,128]{2,1,0:T(8,128)S(1)} %get-tuple-element.15.var, bf16[31,49]{1,0:T(8,128)(2,1)S(1)} %get-tuple-element.16.ct, ...), custom_call_target="tpu_custom_call" | custom-call | tf_op jit(solution)/shard_map/fit/pallas_call | solution.py:459
  17.3 9.2 %all_to_all.11.shares_ref = f32[16,4,128]{2,1,0:T(4,128)S(1)} all-to-all(f32[16,4,128]{2,1,0:T(4,128)S(1)} %get-tuple-element.20), channel_id=1, replica_groups=mesh['group'=2,'visit'=16,'sky'=1] {'visit'}, dimensions={0} | all-to-all | bytes 65536 | tf_op jit(solution)/shard_map/all_to_all | solution.py:575
  26.5 0.6 %results.1 = (f32[1,32,128]{2,1,0:T(8,128)}, f32[1,50]{1,0:T(1,128)}, f32[2,128]{1,0:T(2,128)}) custom-call(f32[16,4,128]{2,1,0:T(4,128)S(1)} %all_to_all.11.shares_ref, f32[1,32,128]{2,1,0:T(8,128)S(1)} %get-tuple-element.21.diff_ref, f32[1,50]{1,0:T(1,128)S(1)} %get-tuple-element.22.coef_ref), custom_call_target="tpu_custom_call" | custom-call | tf_op jit(solution)/shard_map/results/pallas_call | solution.py:547
